TPU v7x, 32 devices: a whole 2x2x4 slice. The times are simulated.
32 devices in a mesh: groups: 2 (over y), feat: 8 (over z, x), corp: 2 (over core).
Axes of the slice: x: 2, y: 2, z: 4, core: 2. Of those that a mesh axis runs over, the one named last changes fastest.
Arguments:
- query_features: bfloat16 [1536, 16384], P(('groups', 'corp'), 'feat'), parts along dimension 0, may hold values from -6 to 6
- inverse_kernel: bfloat16 [16384, 16384], P(None, 'feat'), may hold values from -1 to 3, as said below
- doc_features: bfloat16 [512, 16384], P(('groups', 'corp'), 'feat'), parts along dimension 0, may hold values from -0.046875 to 0.046875
Outputs:
- scores: float32 [1536, 256], P(('groups', 'feat'), 'corp'), parts along dimension 0
There are 2 independent parts, one for each index of `groups`. A program takes and returns all parts, laid end to end along the dimension named above; an argument that names none is the same for every part. Nothing has to cross between parts.
Inputs may be any that keep to these rules, and one draw needn't show every extreme that they name: inverse_kernel is symmetric.
All inputs are finite; a program needn't handle non-finite values.
Results may differ from a plain program's by a relative error of at most 0.0003.
Values may be sent and summed in bfloat16 or wider, within the bound.
No kernel may reach another device: no remote copies, remote signals or barrier semaphores. Data moves between devices by JAX's collectives and lax.ppermute only.
A program may use at most 128 MiB of HBM per device.

v0:
```python
import functools

import jax
import jax.numpy as jnp
from jax import lax
from jax.experimental import pallas as pl
from jax.experimental.pallas import tpu as pltpu
from jax.sharding import PartitionSpec as P


F32 = jnp.float32
BF16 = jnp.bfloat16
SLOTS = 4
TILE_BYTES = 2 << 20


def dot(a, b):
    return jnp.dot(a, b, preferred_element_type=F32)


def dot_t(a, b):
    return lax.dot_general(a, b, (((1,), (1,)), ((), ())), preferred_element_type=F32)


def stream(row_ref, blocks, m_ref, tiles, sems, acc_ref):
    depth = tiles.shape[1]
    counts = [b.shape[1] // depth for b in blocks]
    total = sum(counts)

    def copy(i, start):
        slot = lax.rem(i, SLOTS)
        rows = pl.ds(pl.multiple_of(start, depth), depth)
        return pltpu.make_async_copy(m_ref.at[rows, :], tiles.at[slot], sems.at[slot])

    def start_of(i):
        row = row_ref[0] + i * depth
        base = counts[0]
        for b in range(1, len(blocks)):
            row = jnp.where(i >= base, row_ref[b] + (i - base) * depth, row)
            base += counts[b]
        return row

    for i in range(min(SLOTS, total)):
        copy(i, start_of(i)).start()
    first = 0
    for block, count in zip(blocks, counts):

        def step(j, carry, block=block, first=first):
            i = first + j
            copy(i, 0).wait()
            piece = block[:, pl.ds(pl.multiple_of(j * depth, depth), depth)]
            acc_ref[...] += dot(piece, tiles[lax.rem(i, SLOTS)])

            @pl.when(i + SLOTS < total)
            def _():
                copy(i + SLOTS, start_of(i + SLOTS)).start()

            return carry

        lax.fori_loop(0, count, step, 0)
        first += count


def apply_kernel(n_blocks, has_acc, row_ref, *refs):
    blocks, refs = refs[:n_blocks], refs[n_blocks:]
    m_ref, refs = refs[0], refs[1:]
    if has_acc:
        in_ref, refs = refs[0], refs[1:]
    out_ref, tiles, sems = refs
    out_ref[...] = in_ref[...] if has_acc else jnp.zeros_like(out_ref)
    stream(row_ref, blocks, m_ref, tiles, sems, out_ref)


def score_kernel(n_blocks, n_parts, row_ref, *refs):
    blocks, refs = refs[:n_blocks], refs[n_blocks:]
    m_ref, in_ref, refs = refs[0], refs[1], refs[2:]
    q_refs, (out_ref, acc, tiles, sems) = refs[:n_parts], refs[n_parts:]
    acc[...] = in_ref[...]
    stream(row_ref, blocks, m_ref, tiles, sems, acc)
    hi = acc[...].astype(BF16)
    lo = (acc[...] - hi.astype(F32)).astype(BF16)
    rows = q_refs[0].shape[0]
    for k, q_ref in enumerate(q_refs):
        at = pl.multiple_of(row_ref[n_blocks + k] * rows, rows)
        out_ref[pl.ds(at, rows), :] = dot_t(q_ref[...], hi) + dot_t(q_ref[...], lo)


def tile_depth(m, blocks):
    depth = TILE_BYTES // (m.shape[1] * m.dtype.itemsize)
    return min(depth, *(b.shape[1] for b in blocks))


def call(kernel, rows, operands, specs, out_shape, m, blocks, scratch, extra_flops=0):
    depth = tile_depth(m, blocks)
    width = sum(b.shape[1] for b in blocks)
    vmem = pl.BlockSpec(memory_space=pltpu.VMEM)
    return pl.pallas_call(
        kernel,
        out_shape=out_shape,
        in_specs=[pl.BlockSpec(memory_space=pltpu.SMEM)] + specs,
        out_specs=vmem,
        scratch_shapes=scratch
        + [pltpu.VMEM((SLOTS, depth, m.shape[1]), BF16), pltpu.SemaphoreType.DMA((SLOTS,))],
        cost_estimate=pl.CostEstimate(
            flops=2 * blocks[0].shape[0] * width * m.shape[1] + extra_flops,
            bytes_accessed=2 * width * m.shape[1],
            transcendentals=0,
        ),
        compiler_params=pltpu.CompilerParams(vmem_limit_bytes=32 << 20),
    )(rows, *operands)


VMEM = pl.BlockSpec(memory_space=pltpu.VMEM)
ANY = pl.BlockSpec(memory_space=pl.ANY)


def apply(acc, blocks, rows, m):
    shape = jax.ShapeDtypeStruct((blocks[0].shape[0], m.shape[1]), F32)
    operands = list(blocks) + [m] + ([] if acc is None else [acc])
    specs = [VMEM] * len(blocks) + [ANY] + ([] if acc is None else [VMEM])
    kernel = functools.partial(apply_kernel, len(blocks), acc is not None)
    return call(kernel, jnp.stack(rows), operands, specs, shape, m, blocks, [])


def score(acc, blocks, rows, m, parts, places):
    docs = blocks[0].shape[0]
    queries = sum(p.shape[0] for p in parts)
    shape = jax.ShapeDtypeStruct((queries, docs), F32)
    operands = list(blocks) + [m, acc] + parts
    specs = [VMEM] * len(blocks) + [ANY, VMEM] + [VMEM] * len(parts)
    kernel = functools.partial(score_kernel, len(blocks), len(parts))
    scratch = [pltpu.VMEM(acc.shape, F32)]
    flops = 4 * queries * docs * m.shape[1]
    return call(kernel, jnp.stack(rows + places), operands, specs, shape, m, blocks, scratch, flops)


def scatter_sum(s, n):
    me = lax.axis_index("feat")
    x, z, m = lax.rem(me, 2), lax.div(me, 2), n // 2
    s = s.reshape((m, 2) + s.shape[1:])
    mine = lax.dynamic_index_in_dim(s, x, 1, False)
    theirs = lax.dynamic_index_in_dim(s, 1 - x, 1, False)
    s = mine + lax.ppermute(theirs, "feat", [(i, i ^ 1) for i in range(n)])
    out = lax.dynamic_index_in_dim(s, z, 0, False)
    for k in range(1, m):
        y = lax.dynamic_index_in_dim(s, lax.rem(z + k, m), 0, False)
        out = out + lax.ppermute(y, "feat", [(i, (i + 2 * k) % n) for i in range(n)])
    return out


def ring_body(n, n_corp, q, m, d):
    docs, width = d.shape
    half = width // 2
    far = n // 2
    order = list(range(0, n, 2)) + list(range(n - 1, 0, -2))

    def turn(x, k):
        return lax.ppermute(x, "feat", [(order[p], order[(p + k) % n]) for p in range(n)])

    table = [[order[(order.index(f) + k) % n] * width for k in range(n)] for f in range(n)]
    starts = jnp.array(table, jnp.int32)[lax.axis_index("feat")]

    def at(k):
        return starts[k % n]

    core = lax.axis_index("corp")
    up, down = turn(d, 1), turn(d, -1)
    parts = [q] + [
        lax.ppermute(q, "corp", [(i, (i + k) % n_corp) for i in range(n_corp)]) for k in range(1, n_corp)
    ]
    places = [lax.rem(core + n_corp - k, n_corp) for k in range(n_corp)]
    acc = apply(None, [d], [at(0)], m)
    for s in range(1, far - 1):
        if s < far - 2:
            new_up, new_down = turn(up, 1), turn(down, -1)
        else:
            up_a, down_a = turn(up[:, :half], 1), turn(down[:, half:], -1)
            up_b, down_b = turn(up[:, half:], 1), turn(down[:, :half], -1)
        acc = apply(acc, [up, down], [at(-s), at(s)], m)
        if s < far - 2:
            up, down = new_up, new_down
    s = far - 1
    up_z, down_z = turn(up_a, 1), turn(down_a, -1)
    acc = apply(acc, [up_a, down_a], [at(-s), at(s) + half], m)
    acc = apply(acc, [up_b, down_b], [at(-s) + half, at(s)], m)
    scores = score(acc, [up_z, down_z], [at(far), at(far) + half], m, parts, places)
    return scatter_sum(scores.reshape(n, -1, docs), n)


def plain_body(q, m, d):
    applied = dot(lax.all_gather(d, "feat", axis=1, tiled=True), m)
    left = lax.all_gather(q, "corp", axis=0, tiled=True).astype(F32)
    scores = lax.dot_general(
        left, applied, (((1,), (1,)), ((), ())), precision=lax.Precision.HIGHEST, preferred_element_type=F32
    )
    return lax.psum_scatter(scores, "feat", scatter_dimension=0, tiled=True)


def solution(mesh):
    n, n_corp = mesh.shape["feat"], mesh.shape["corp"]
    ring = n % 4 == 0 and 8 <= n <= 16

    def on_device(q, m, d):
        if not ring:
            return plain_body(q, m, d)
        return ring_body(n, n_corp, q, m, d)

    placed = (P(("groups", "corp"), "feat"), P(None, "feat"), P(("groups", "corp"), "feat"))
    return jax.shard_map(
        on_device,
        mesh=mesh,
        in_specs=placed,
        out_specs=P(("groups", "feat"), "corp"),
        check_vma=False,
    )
```

profile of v0, /device:TPU:0, one launch (start us, length us, event | category | flops | bytes accessed | tf_op | source)
XLA Modules:
  0.0 87.6 jit_solution(1010541347153958983)
XLA Ops:
  0.0 3.1 %collective-permute-start = (bf16[128,2048]{1,0:T(8,128)(2,1)}, bf16[128,2048]{1,0:T(8,128)(2,1)}, u32[]{:S(2)}, u32[]{:S(2)}) collective-permute-start(bf16[128,2048]{1,0:T(8,128)(2,1)} %refs_0_.1), channel_id=1, source_target_pairs={{0,4},{4,8},{8,12},{12,14},{14,10},{10,6},{6,2},{2,0},{1,5},{5,9},... | collective-permute-start | bytes 1572872 | tf_op jit(solution)/shard_map/ppermute | solution.py:158
  3.1 0.7 constant_dynamic-slice_fusion
  3.8 0.7 fusion.4
  4.4 10.9 %collective-permute-done.refs_0_ = bf16[128,2048]{1,0:T(8,128)(2,1)} collective-permute-done((bf16[128,2048]{1,0:T(8,128)(2,1)}, bf16[128,2048]{1,0:T(8,128)(2,1)}, u32[]{:S(2)}, u32[]{:S(2)}) %collective-permute-start) | collective-permute-done | bytes 524320 | tf_op jit(solution)/shard_map/ppermute | solution.py:158
  15.3 1.8 %collective-permute-start.1 = (bf16[128,2048]{1,0:T(8,128)(2,1)}, bf16[128,2048]{1,0:T(8,128)(2,1)S(1)}, u32[]{:S(2)}, u32[]{:S(2)}) collective-permute-start(bf16[128,2048]{1,0:T(8,128)(2,1)} %collective-permute-done.refs_0_), channel_id=1, source_target_pairs={{0,4},{4,8},{8,12},{12,14},{14,10},{10,6},{6,2},{2,0},{1,5},{5,9},... | collective-permute-start | bytes 1572872 | tf_op jit(solution)/shard_map/ppermute | solution.py:158
  17.0 1.4 %pad_add_fusion.4.row_ref = s32[2]{0:T(128)S(1)} fusion(s32[1]{0:T(128)} %bitcast.11, s32[1]{0:T(128)} %bitcast.10), kind=kLoop, calls=%fused_computation.13 | loop fusion | flops 2 | bytes 16 | tf_op jit(solution)/shard_map/stack | solution.py:122
  18.4 1.3 %pad_add_fusion.3.row_ref = s32[2]{0:T(128)S(1)} fusion(s32[1]{0:T(128)} %bitcast.9, s32[1]{0:T(128)} %bitcast.8), kind=kLoop, calls=%fused_computation.12 | loop fusion | flops 2 | bytes 16 | tf_op jit(solution)/shard_map/stack | solution.py:122
  20.7 0.7 pad_add_fusion.2.row_ref
  22.6 0.7 pad_add_fusion.1.row_ref
  23.4 0.6 pad_add_fusion.row_ref
  24.0 4.6 %collective-permute-done.1.refs_0_ = bf16[128,2048]{1,0:T(8,128)(2,1)S(1)} collective-permute-done((bf16[128,2048]{1,0:T(8,128)(2,1)}, bf16[128,2048]{1,0:T(8,128)(2,1)S(1)}, u32[]{:S(2)}, u32[]{:S(2)}) %collective-permute-start.1) | collective-permute-done | bytes 524320 | tf_op jit(solution)/shard_map/ppermute | solution.py:158
  28.6 1.5 %collective-permute-start.2 = (bf16[128,1024]{1,0:T(8,128)(2,1)S(1)}, bf16[128,1024]{1,0:T(8,128)(2,1)S(1)}, u32[]{:S(2)}, u32[]{:S(2)}) collective-permute-start(bf16[128,1024]{1,0:T(8,128)(2,1)S(1)} %get-tuple-element.8), channel_id=1, source_target_pairs={{0,4},{4,8},{8,12},{12,14},{14,10},{10,6},{6,2},{2,0},{1,5},{5,9},... | collective-permute-start | bytes 786440 | tf_op jit(solution)/shard_map/ppermute | solution.py:158
  30.1 3.0 %collective-permute-done.5.refs_1_ = bf16[128,2048]{1,0:T(8,128)(2,1)S(1)} collective-permute-done((bf16[128,2048]{1,0:T(8,128)(2,1)}, bf16[128,2048]{1,0:T(8,128)(2,1)S(1)}, u32[]{:S(2)}, u32[]{:S(2)}) %collective-permute-start.5) | collective-permute-done | bytes 524320 | tf_op jit(solution)/shard_map/ppermute | solution.py:158
  33.2 0.6 collective-permute-start.6
  33.8 4.6 %shard_map.46.refs_3_ = f32[128,2048]{1,0:T(8,128)S(1)} custom-call(s32[1]{0:T(128)} %bitcast.12.row_ref, bf16[128,2048]{1,0:T(8,128)(2,1)S(1)} %copy-done.1, bf16[16384,2048]{1,0:T(8,128)(2,1)} %refs_2_.9), custom_call_target="tpu_custom_call" | custom-call | flops 1073741824 | bytes 8388608 | tf_op jit(solution)/shard_map/pallas_call | solution.py:97
  38.4 7.8 %shard_map.47.refs_3_ = f32[128,2048]{1,0:T(8,128)S(1)} custom-call(s32[2]{0:T(128)S(1)} %pad_add_fusion.4.row_ref, bf16[128,2048]{1,0:T(8,128)(2,1)} %collective-permute-done.refs_0_, bf16[128,2048]{1,0:T(8,128)(2,1)} %collective-permute-done.4.refs_1_, bf16[16384,2048]{1,0:T(8,128)(2,1)} %refs_2_.9, f32[128,2048]{1,0:T(8,128)S(1)} %shard_map.46.refs_3_), custom_call_target="tpu_custom_call" | custom-call | flops 2147483648 | bytes 16777216 | tf_op jit(solution)/shard_map/pallas_call | solution.py:97
  46.2 1.5 %collective-permute-start.8 = (bf16[128,1024]{1,0:T(8,128)(2,1)S(1)}, bf16[128,1024]{1,0:T(8,128)(2,1)S(1)}, u32[]{:S(2)}, u32[]{:S(2)}) collective-permute-start(bf16[128,1024]{1,0:T(8,128)(2,1)S(1)} %get-tuple-element.7), channel_id=1, source_target_pairs={{0,4},{4,8},{8,12},{12,14},{14,10},{10,6},{6,2},{2,0},{1,5},{5,9},... | collective-permute-start | bytes 786440 | tf_op jit(solution)/shard_map/ppermute | solution.py:158
  47.8 0.5 collective-permute-start.9
  48.3 1.5 %collective-permute-start.3 = (bf16[128,1024]{1,0:T(8,128)(2,1)S(1)}, bf16[128,1024]{1,0:T(8,128)(2,1)S(1)}, u32[]{:S(2)}, u32[]{:S(2)}) collective-permute-start(bf16[128,1024]{1,0:T(8,128)(2,1)S(1)} %collective-permute-done.2.refs_0_), channel_id=1, source_target_pairs={{0,4},{4,8},{8,12},{12,14},{14,10},{10,6},{6,2},{2,0},{1,5},{5,9},... | collective-permute-start | bytes 786440 | tf_op jit(solution)/shard_map/ppermute | solution.py:158
  49.8 0.5 collective-permute-start.7
  50.3 7.1 %shard_map.48.refs_3_ = f32[128,2048]{1,0:T(8,128)S(1)} custom-call(s32[2]{0:T(128)S(1)} %pad_add_fusion.3.row_ref, bf16[128,2048]{1,0:T(8,128)(2,1)S(1)} %collective-permute-done.1.refs_0_, bf16[128,2048]{1,0:T(8,128)(2,1)S(1)} %collective-permute-done.5.refs_1_, bf16[16384,2048]{1,0:T(8,128)(2,1)} %refs_2_.9, f32[128,2048]{1,0:T(8,128)S(1)} %shard_map.47.refs_3_), custom_call_target="tpu_custom_call" | custom-call | flops 2147483648 | bytes 16777216 | tf_op jit(solution)/shard_map/pallas_call | solution.py:97
  57.5 4.5 %shard_map.49.refs_3_ = f32[128,2048]{1,0:T(8,128)S(1)} custom-call(s32[2]{0:T(128)S(1)} %pad_add_fusion.2.row_ref, bf16[128,1024]{1,0:T(8,128)(2,1)S(1)} %collective-permute-done.2.refs_0_, bf16[128,1024]{1,0:T(8,128)(2,1)S(1)} %collective-permute-done.6.refs_1_, bf16[16384,2048]{1,0:T(8,128)(2,1)} %refs_2_.9, f32[128,2048]{1,0:T(8,128)S(1)} %shard_map.48.refs_3_), custom_call_target="tpu_custom_call" | custom-call | flops 1073741824 | bytes 8388608 | tf_op jit(solution)/shard_map/pallas_call | solution.py:97
  62.0 4.5 %shard_map.50.refs_3_ = f32[128,2048]{1,0:T(8,128)S(1)} custom-call(s32[2]{0:T(128)S(1)} %pad_add_fusion.1.row_ref, bf16[128,1024]{1,0:T(8,128)(2,1)S(1)} %collective-permute-done.8.refs_0_, bf16[128,1024]{1,0:T(8,128)(2,1)S(1)} %collective-permute-done.9.refs_1_, bf16[16384,2048]{1,0:T(8,128)(2,1)} %refs_2_.9, f32[128,2048]{1,0:T(8,128)S(1)} %shard_map.49.refs_3_), custom_call_target="tpu_custom_call" | custom-call | flops 1073741824 | bytes 8388608 | tf_op jit(solution)/shard_map/pallas_call | solution.py:97
  66.6 6.3 %shard_map.51 = f32[768,128]{1,0:T(8,128)S(1)} custom-call(s32[4]{0:T(128)S(1)} %pad_add_fusion.row_ref, bf16[128,1024]{1,0:T(8,128)(2,1)S(1)} %collective-permute-done.3.refs_0_, bf16[128,1024]{1,0:T(8,128)(2,1)S(1)} %collective-permute-done.7.refs_1_, bf16[16384,2048]{1,0:T(8,128)(2,1)} %refs_2_.9, f32[128,2048]{1,0:T(8,128)S(1)} %shard_map.50.refs_3_, ...), custom_call_target="tpu_custom_call" | custom-call | flops 1879048192 | bytes 8388608 | tf_op jit(solution)/shard_map/pallas_call | solution.py:97
  73.0 1.5 %collective-permute-start.11 = (f32[4,96,128]{2,1,0:T(8,128)S(1)}, f32[4,96,128]{2,1,0:T(8,128)S(1)}, u32[]{:S(2)}, u32[]{:S(2)}) collective-permute-start(f32[4,96,128]{2,1,0:T(8,128)S(1)} %dynamic-slice_bitcast_fusion), channel_id=1, source_target_pairs={{0,2},{2,0},{4,6},{6,4},{8,10},{10,8},{12,14},{14,12},{1,3},{3,1},... | collective-permute-start | bytes 589832 | tf_op jit(solution)/shard_map/ppermute | solution.py:143
  74.4 4.3 %collective-permute-done.11 = f32[4,96,128]{2,1,0:T(8,128)S(1)} collective-permute-done((f32[4,96,128]{2,1,0:T(8,128)S(1)}, f32[4,96,128]{2,1,0:T(8,128)S(1)}, u32[]{:S(2)}, u32[]{:S(2)}) %collective-permute-start.11) | collective-permute-done | bytes 196640 | tf_op jit(solution)/shard_map/ppermute | solution.py:143
  78.8 1.5 %collective-permute-start.12 = (f32[96,128]{1,0:T(8,128)S(1)}, f32[96,128]{1,0:T(8,128)S(1)}, u32[]{:S(2)}, u32[]{:S(2)}) collective-permute-start(f32[96,128]{1,0:T(8,128)S(1)} %get-tuple-element.9), channel_id=1, source_target_pairs={{0,4},{2,6},{4,8},{6,10},{8,12},{10,14},{12,0},{14,2},{1,5},{3,7},... | collective-permute-start | bytes 147464 | tf_op jit(solution)/shard_map/ppermute | solution.py:147
  80.3 2.6 %collective-permute-start.13 = (f32[96,128]{1,0:T(8,128)S(1)}, f32[96,128]{1,0:T(8,128)S(1)}, u32[]{:S(2)}, u32[]{:S(2)}) collective-permute-start(f32[96,128]{1,0:T(8,128)S(1)} %get-tuple-element.11), channel_id=1, source_target_pairs={{0,8},{2,10},{4,12},{6,14},{8,0},{10,2},{12,4},{14,6},{1,9},{3,11}... | collective-permute-start | bytes 147464 | tf_op jit(solution)/shard_map/ppermute | solution.py:147
  82.9 1.3 %collective-permute-start.14 = (f32[96,128]{1,0:T(8,128)S(1)}, f32[96,128]{1,0:T(8,128)S(1)}, u32[]{:S(2)}, u32[]{:S(2)}) collective-permute-start(f32[96,128]{1,0:T(8,128)S(1)} %get-tuple-element.10), channel_id=1, source_target_pairs={{0,12},{2,14},{4,0},{6,2},{8,4},{10,6},{12,8},{14,10},{1,13},{3,15... | collective-permute-start | bytes 147464 | tf_op jit(solution)/shard_map/ppermute | solution.py:147
  84.7 0.6 collective-permute-done.13
  85.3 1.7 %collective-permute-done.14 = f32[96,128]{1,0:T(8,128)S(1)} collective-permute-done((f32[96,128]{1,0:T(8,128)S(1)}, f32[96,128]{1,0:T(8,128)S(1)}, u32[]{:S(2)}, u32[]{:S(2)}) %collective-permute-start.14) | collective-permute-done | bytes 49184 | tf_op jit(solution)/shard_map/ppermute | solution.py:147
  87.0 0.6 fusion.1
  (21 shorter events, 1.0 us)
Async XLA Ops:
  0.0 33.8 %copy-start.1 = (bf16[128,2048]{1,0:T(8,128)(2,1)S(1)}, bf16[128,2048]{1,0:T(8,128)(2,1)}, u32[]{:S(2)}) copy-start(bf16[128,2048]{1,0:T(8,128)(2,1)} %refs_0_.1) | copy-start | bytes 1572868
  0.0 15.3 %collective-permute-start = (bf16[128,2048]{1,0:T(8,128)(2,1)}, bf16[128,2048]{1,0:T(8,128)(2,1)}, u32[]{:S(2)}, u32[]{:S(2)}) collective-permute-start(bf16[128,2048]{1,0:T(8,128)(2,1)} %refs_0_.1), channel_id=1, source_target_pairs={{0,4},{4,8},{8,12},{12,14},{14,10},{10,6},{6,2},{2,0},{1,5},{5,9},... | collective-permute-start | bytes 1572872 | tf_op jit(solution)/shard_map/ppermute | solution.py:158
  3.1 17.3 %collective-permute-start.4 = (bf16[128,2048]{1,0:T(8,128)(2,1)}, bf16[128,2048]{1,0:T(8,128)(2,1)}, u32[]{:S(2)}, u32[]{:S(2)}) collective-permute-start(bf16[128,2048]{1,0:T(8,128)(2,1)} %refs_0_.1), channel_id=1, source_target_pairs={{0,2},{4,0},{8,4},{12,8},{14,12},{10,14},{6,10},{2,6},{1,3},{5,1},... | collective-permute-start | bytes 1572872 | tf_op jit(solution)/shard_map/ppermute | solution.py:158
  3.1 63.5 %collective-permute-start.10 = (bf16[384,2048]{1,0:T(8,128)(2,1)}, bf16[384,2048]{1,0:T(8,128)(2,1)S(1)}, u32[]{:S(2)}, u32[]{:S(2)}) collective-permute-start(bf16[384,2048]{1,0:T(8,128)(2,1)} %refs_4_.1), channel_id=1, source_target_pairs={{0,1},{1,0},{2,3},{3,2},{4,5},{5,4},{6,7},{7,6},{8,9},{9,8},{10,11... | collective-permute-start | bytes 4718600 | tf_op jit(solution)/shard_map/ppermute | solution.py:169
  15.3 13.3 %collective-permute-start.1 = (bf16[128,2048]{1,0:T(8,128)(2,1)}, bf16[128,2048]{1,0:T(8,128)(2,1)S(1)}, u32[]{:S(2)}, u32[]{:S(2)}) collective-permute-start(bf16[128,2048]{1,0:T(8,128)(2,1)} %collective-permute-done.refs_0_), channel_id=1, source_target_pairs={{0,4},{4,8},{8,12},{12,14},{14,10},{10,6},{6,2},{2,0},{1,5},{5,9},... | collective-permute-start | bytes 1572872 | tf_op jit(solution)/shard_map/ppermute | solution.py:158
  20.4 12.8 %collective-permute-start.5 = (bf16[128,2048]{1,0:T(8,128)(2,1)}, bf16[128,2048]{1,0:T(8,128)(2,1)S(1)}, u32[]{:S(2)}, u32[]{:S(2)}) collective-permute-start(bf16[128,2048]{1,0:T(8,128)(2,1)} %collective-permute-done.4.refs_1_), channel_id=1, source_target_pairs={{0,2},{4,0},{8,4},{12,8},{14,12},{10,14},{6,10},{2,6},{1,3},{5,1},... | collective-permute-start | bytes 1572872 | tf_op jit(solution)/shard_map/ppermute | solution.py:158
  28.6 19.7 %collective-permute-start.2 = (bf16[128,1024]{1,0:T(8,128)(2,1)S(1)}, bf16[128,1024]{1,0:T(8,128)(2,1)S(1)}, u32[]{:S(2)}, u32[]{:S(2)}) collective-permute-start(bf16[128,1024]{1,0:T(8,128)(2,1)S(1)} %get-tuple-element.8), channel_id=1, source_target_pairs={{0,4},{4,8},{8,12},{12,14},{14,10},{10,6},{6,2},{2,0},{1,5},{5,9},... | collective-permute-start | bytes 786440 | tf_op jit(solution)/shard_map/ppermute | solution.py:158
  33.2 16.6 %collective-permute-start.6 = (bf16[128,1024]{1,0:T(8,128)(2,1)S(1)}, bf16[128,1024]{1,0:T(8,128)(2,1)S(1)}, u32[]{:S(2)}, u32[]{:S(2)}) collective-permute-start(bf16[128,1024]{1,0:T(8,128)(2,1)S(1)} %get-tuple-element.6), channel_id=1, source_target_pairs={{0,2},{4,0},{8,4},{12,8},{14,12},{10,14},{6,10},{2,6},{1,3},{5,1},... | collective-permute-start | bytes 786440 | tf_op jit(solution)/shard_map/ppermute | solution.py:158
  46.2 15.8 %collective-permute-start.8 = (bf16[128,1024]{1,0:T(8,128)(2,1)S(1)}, bf16[128,1024]{1,0:T(8,128)(2,1)S(1)}, u32[]{:S(2)}, u32[]{:S(2)}) collective-permute-start(bf16[128,1024]{1,0:T(8,128)(2,1)S(1)} %get-tuple-element.7), channel_id=1, source_target_pairs={{0,4},{4,8},{8,12},{12,14},{14,10},{10,6},{6,2},{2,0},{1,5},{5,9},... | collective-permute-start | bytes 786440 | tf_op jit(solution)/shard_map/ppermute | solution.py:158
  47.8 14.3 %collective-permute-start.9 = (bf16[128,1024]{1,0:T(8,128)(2,1)S(1)}, bf16[128,1024]{1,0:T(8,128)(2,1)S(1)}, u32[]{:S(2)}, u32[]{:S(2)}) collective-permute-start(bf16[128,1024]{1,0:T(8,128)(2,1)S(1)} %get-tuple-element.5), channel_id=1, source_target_pairs={{0,2},{4,0},{8,4},{12,8},{14,12},{10,14},{6,10},{2,6},{1,3},{5,1},... | collective-permute-start | bytes 786440 | tf_op jit(solution)/shard_map/ppermute | solution.py:158
  48.3 18.3 %collective-permute-start.3 = (bf16[128,1024]{1,0:T(8,128)(2,1)S(1)}, bf16[128,1024]{1,0:T(8,128)(2,1)S(1)}, u32[]{:S(2)}, u32[]{:S(2)}) collective-permute-start(bf16[128,1024]{1,0:T(8,128)(2,1)S(1)} %collective-permute-done.2.refs_0_), channel_id=1, source_target_pairs={{0,4},{4,8},{8,12},{12,14},{14,10},{10,6},{6,2},{2,0},{1,5},{5,9},... | collective-permute-start | bytes 786440 | tf_op jit(solution)/shard_map/ppermute | solution.py:158
  49.8 16.8 %collective-permute-start.7 = (bf16[128,1024]{1,0:T(8,128)(2,1)S(1)}, bf16[128,1024]{1,0:T(8,128)(2,1)S(1)}, u32[]{:S(2)}, u32[]{:S(2)}) collective-permute-start(bf16[128,1024]{1,0:T(8,128)(2,1)S(1)} %collective-permute-done.6.refs_1_), channel_id=1, source_target_pairs={{0,2},{4,0},{8,4},{12,8},{14,12},{10,14},{6,10},{2,6},{1,3},{5,1},... | collective-permute-start | bytes 786440 | tf_op jit(solution)/shard_map/ppermute | solution.py:158
  62.0 4.6 %copy-start = (bf16[384,2048]{1,0:T(8,128)(2,1)S(1)}, bf16[384,2048]{1,0:T(8,128)(2,1)}, u32[]{:S(2)}) copy-start(bf16[384,2048]{1,0:T(8,128)(2,1)} %refs_4_.1) | copy-start | bytes 4718596
  73.0 5.7 %collective-permute-start.11 = (f32[4,96,128]{2,1,0:T(8,128)S(1)}, f32[4,96,128]{2,1,0:T(8,128)S(1)}, u32[]{:S(2)}, u32[]{:S(2)}) collective-permute-start(f32[4,96,128]{2,1,0:T(8,128)S(1)} %dynamic-slice_bitcast_fusion), channel_id=1, source_target_pairs={{0,2},{2,0},{4,6},{6,4},{8,10},{10,8},{12,14},{14,12},{1,3},{3,1},... | collective-permute-start | bytes 589832 | tf_op jit(solution)/shard_map/ppermute | solution.py:143
  78.8 5.9 %collective-permute-start.12 = (f32[96,128]{1,0:T(8,128)S(1)}, f32[96,128]{1,0:T(8,128)S(1)}, u32[]{:S(2)}, u32[]{:S(2)}) collective-permute-start(f32[96,128]{1,0:T(8,128)S(1)} %get-tuple-element.9), channel_id=1, source_target_pairs={{0,4},{2,6},{4,8},{6,10},{8,12},{10,14},{12,0},{14,2},{1,5},{3,7},... | collective-permute-start | bytes 147464 | tf_op jit(solution)/shard_map/ppermute | solution.py:147
  80.3 5.0 %collective-permute-start.13 = (f32[96,128]{1,0:T(8,128)S(1)}, f32[96,128]{1,0:T(8,128)S(1)}, u32[]{:S(2)}, u32[]{:S(2)}) collective-permute-start(f32[96,128]{1,0:T(8,128)S(1)} %get-tuple-element.11), channel_id=1, source_target_pairs={{0,8},{2,10},{4,12},{6,14},{8,0},{10,2},{12,4},{14,6},{1,9},{3,11}... | collective-permute-start | bytes 147464 | tf_op jit(solution)/shard_map/ppermute | solution.py:147
  82.9 4.1 %collective-permute-start.14 = (f32[96,128]{1,0:T(8,128)S(1)}, f32[96,128]{1,0:T(8,128)S(1)}, u32[]{:S(2)}, u32[]{:S(2)}) collective-permute-start(f32[96,128]{1,0:T(8,128)S(1)} %get-tuple-element.10), channel_id=1, source_target_pairs={{0,12},{2,14},{4,0},{6,2},{8,4},{10,6},{12,8},{14,10},{1,13},{3,15... | collective-permute-start | bytes 147464 | tf_op jit(solution)/shard_map/ppermute | solution.py:147
where the time goes:
time: 87.9 us; the launch traced here: 87.6 us
  Pallas kernels  34.9 us (40%)
  waiting for transfers between devices  25.5 us (29%)
  starting transfers between devices  18.3 us (21%)
  other arithmetic  5.39 us (6%)
  between operations  2.03 us (2%)
  local copies, waits for them, and re-layouts  1.48 us (2%)
    pallas_call x6, Pallas kernels, call(): pl.pallas_call(kernel, out_shape=out_shape, in_specs=[pl.BlockSpec(memory...  34.9 us
    ppermute x10, waiting for transfers between devices, turn(): lax.ppermute(x, 'feat', [(order[p], order[(p + k) % n]) for p in range(n)])  18.5 us
    ppermute x10, starting transfers between devices, turn(): lax.ppermute(x, 'feat', [(order[p], order[(p + k) % n]) for p in range(n)])  11.4 us
    ppermute x3, starting transfers between devices, scatter_sum(): lax.ppermute(y, 'feat', [(i, (i + 2 * k) % n) for i in range(n)])  5.46 us
    ppermute x1, waiting for transfers between devices, scatter_sum(): s = mine + lax.ppermute(theirs, 'feat', [(i, i ^ 1) for i in range(n)])  4.28 us
    another operation x4, other arithmetic, apply(): return call(kernel, jnp.stack(rows), operands, specs, shape, m, blocks, [])  4.11 us
    ppermute x3, waiting for transfers between devices, scatter_sum(): lax.ppermute(y, 'feat', [(i, (i + 2 * k) % n) for i in range(n)])  2.74 us
  transfers between devices with their start and end apart: 15, of which 7 were waited for; matrix products, arithmetic and copies ran while one was open for 7% of the time, Pallas kernels for 33%

commit v1 on v0

v1 whole, which is shorter than its diff:
```python
import functools

import jax
import jax.numpy as jnp
from jax import lax
from jax.experimental import pallas as pl
from jax.experimental.pallas import tpu as pltpu
from jax.sharding import PartitionSpec as P


F32 = jnp.float32
BF16 = jnp.bfloat16
SLOTS = 6
TILE_ROWS = 512


def dot(a, b):
    return jnp.dot(a, b, preferred_element_type=F32)


def dot_t(a, b):
    return lax.dot_general(a, b, (((1,), (1,)), ((), ())), preferred_element_type=F32)


def ring_order(n):
    return list(range(0, n, 2)) + list(range(n - 1, 0, -2))


def ring_owner(n, k):
    me = lax.axis_index("feat")
    place = jnp.where(lax.rem(me, 2) == 0, lax.div(me, 2), n - 1 - lax.div(me, 2))
    place = lax.rem(place + (k + n) % n, n)
    return jnp.where(place < n // 2, 2 * place, 2 * (n - 1 - place) + 1)


def stream(n, rows, blocks, m_ref, tiles, sems, acc_ref):
    slots, depth, width = tiles.shape
    counts = [b.shape[1] // depth for b in blocks]
    total = sum(counts)
    starts = [ring_owner(n, k) * width + first for k, first in rows]

    def copy(i, start):
        slot = lax.rem(i, slots)
        at = pl.ds(pl.multiple_of(start, depth), depth)
        return pltpu.make_async_copy(m_ref.at[at, :], tiles.at[slot], sems.at[slot])

    def start_of(i):
        row, base = starts[0] + i * depth, counts[0]
        for b in range(1, len(blocks)):
            row = jnp.where(i >= base, starts[b] + (i - base) * depth, row)
            base += counts[b]
        return row

    for i in range(min(slots, total)):
        copy(i, start_of(i)).start()
    first = 0
    for block, count in zip(blocks, counts):

        def step(j, carry, block=block, first=first):
            i = first + j
            copy(i, 0).wait()
            piece = block[:, pl.ds(pl.multiple_of(j * depth, depth), depth)]
            acc_ref[...] += dot(piece, tiles[lax.rem(i, slots)])

            @pl.when(i + slots < total)
            def _():
                copy(i + slots, start_of(i + slots)).start()

            return carry

        lax.fori_loop(0, count, step, 0)
        first += count


def apply_kernel(n, rows, has_acc, *refs):
    blocks, refs = refs[: len(rows)], refs[len(rows) :]
    m_ref, out_ref, tiles, sems = refs[0], refs[-3], refs[-2], refs[-1]
    if not has_acc:
        out_ref[...] = jnp.zeros_like(out_ref)
    stream(n, rows, blocks, m_ref, tiles, sems, out_ref)


def score_kernel(n, rows, n_parts, *refs):
    blocks, refs = refs[: len(rows)], refs[len(rows) :]
    m_ref, in_ref, refs = refs[0], refs[1], refs[2:]
    q_refs, (out_ref, acc, pair, tiles, sems) = refs[:n_parts], refs[n_parts:]
    acc[...] = in_ref[...]
    stream(n, rows, blocks, m_ref, tiles, sems, acc)
    docs = acc.shape[0]
    hi = acc[...].astype(BF16)
    pair[:docs, :] = hi
    pair[docs:, :] = (acc[...] - hi.astype(F32)).astype(BF16)
    count = q_refs[0].shape[0]
    for k, q_ref in enumerate(q_refs):
        place = lax.rem(lax.axis_index("corp") + n_parts - k, n_parts)
        both = dot_t(q_ref[...], pair[...])
        out_ref[pl.ds(pl.multiple_of(place * count, count), count), :] = both[:, :docs] + both[:, docs:]


def call(kernel, operands, out_shape, m, blocks, scratch, extra_flops=0, aliases=None):
    depth = min(TILE_ROWS, *(b.shape[1] for b in blocks))
    width = sum(b.shape[1] for b in blocks)
    return pl.pallas_call(
        kernel,
        out_shape=out_shape,
        in_specs=[pl.BlockSpec(memory_space=pl.ANY if x is m else pltpu.VMEM) for x in operands],
        out_specs=pl.BlockSpec(memory_space=pltpu.VMEM),
        scratch_shapes=scratch
        + [pltpu.VMEM((SLOTS, depth, m.shape[1]), BF16), pltpu.SemaphoreType.DMA((SLOTS,))],
        input_output_aliases=aliases or {},
        cost_estimate=pl.CostEstimate(
            flops=2 * blocks[0].shape[0] * width * m.shape[1] + extra_flops,
            bytes_accessed=2 * width * m.shape[1],
            transcendentals=0,
        ),
        compiler_params=pltpu.CompilerParams(vmem_limit_bytes=32 << 20),
    )(*operands)


def apply(n, acc, blocks, rows, m):
    shape = jax.ShapeDtypeStruct((blocks[0].shape[0], m.shape[1]), F32)
    operands = list(blocks) + [m] + ([] if acc is None else [acc])
    kernel = functools.partial(apply_kernel, n, rows, acc is not None)
    return call(kernel, operands, shape, m, blocks, [], aliases=None if acc is None else {len(blocks) + 1: 0})


def score(n, acc, blocks, rows, m, parts):
    docs = blocks[0].shape[0]
    queries = sum(p.shape[0] for p in parts)
    shape = jax.ShapeDtypeStruct((queries, docs), F32)
    kernel = functools.partial(score_kernel, n, rows, len(parts))
    scratch = [pltpu.VMEM(acc.shape, F32), pltpu.VMEM((2 * docs, m.shape[1]), BF16)]
    flops = 4 * queries * docs * m.shape[1]
    return call(kernel, list(blocks) + [m, acc] + parts, shape, m, blocks, scratch, flops)


def scatter_sum(s, n):
    me = lax.axis_index("feat")
    x, z, m = lax.rem(me, 2), lax.div(me, 2), n // 2
    s = s.reshape((m, 2) + s.shape[1:])
    mine = lax.dynamic_index_in_dim(s, x, 1, False)
    theirs = lax.dynamic_index_in_dim(s, 1 - x, 1, False)
    s = mine + lax.ppermute(theirs, "feat", [(i, i ^ 1) for i in range(n)])
    out = lax.dynamic_index_in_dim(s, z, 0, False)
    for k in range(1, m):
        y = lax.dynamic_index_in_dim(s, lax.rem(z + k, m), 0, False)
        out = out + lax.ppermute(y, "feat", [(i, (i + 2 * k) % n) for i in range(n)])
    return out


def ring_body(n, n_corp, q, m, d):
    docs, width = d.shape
    half = width // 2
    far = n // 2
    order = ring_order(n)

    def turn(x, k):
        return lax.ppermute(x, "feat", [(order[p], order[(p + k) % n]) for p in range(n)])

    def run(*args):
        return apply(n, *args, m)

    up, down = turn(d, 1), turn(d, -1)
    parts = [q] + [lax.ppermute(q, "corp", [(i, (i + k) % n_corp) for i in range(n_corp)]) for k in range(1, n_corp)]
    acc = run(None, [d], [(0, 0)])
    for s in range(1, far - 1):
        if s < far - 2:
            new_up, new_down = turn(up, 1), turn(down, -1)
        else:
            up_a, down_a = turn(up[:, :half], 1), turn(down[:, half:], -1)
            up_b, down_b = turn(up[:, half:], 1), turn(down[:, :half], -1)
        acc = run(acc, [up, down], [(-s, 0), (s, 0)])
        if s < far - 2:
            up, down = new_up, new_down
    s = far - 1
    up_z, down_z = turn(up_a, 1), turn(down_a, -1)
    acc = run(acc, [up_a, down_a, up_b, down_b], [(-s, 0), (s, half), (-s, half), (s, 0)])
    scores = score(n, acc, [up_z, down_z], [(far, 0), (far, half)], m, parts)
    return scatter_sum(scores.reshape(n, -1, docs), n)


def plain_body(q, m, d):
    applied = dot(lax.all_gather(d, "feat", axis=1, tiled=True), m)
    left = lax.all_gather(q, "corp", axis=0, tiled=True).astype(F32)
    scores = lax.dot_general(
        left, applied, (((1,), (1,)), ((), ())), precision=lax.Precision.HIGHEST, preferred_element_type=F32
    )
    return lax.psum_scatter(scores, "feat", scatter_dimension=0, tiled=True)


def solution(mesh):
    n, n_corp = mesh.shape["feat"], mesh.shape["corp"]
    ring = n % 4 == 0 and 8 <= n <= 16

    def on_device(q, m, d):
        if not ring:
            return plain_body(q, m, d)
        return ring_body(n, n_corp, q, m, d)

    placed = (P(("groups", "corp"), "feat"), P(None, "feat"), P(("groups", "corp"), "feat"))
    return jax.shard_map(
        on_device,
        mesh=mesh,
        in_specs=placed,
        out_specs=P(("groups", "feat"), "corp"),
        check_vma=False,
    )
```

time: 87.9 us -> 81.5 us (0.927)
  waiting for transfers between devices: 25.5 us -> 31.7 us
  Pallas kernels: 34.9 us -> 30.1 us
  other arithmetic: 5.39 us -> 0.66 us
  between operations: 2.03 us -> 0.15 us
  local copies, waits for them, and re-layouts: 1.48 us -> 0.12 us
    ppermute x10, waiting for transfers between devices: 18.5 us -> 24.9 us  [turn(): lax.ppermute(x, 'feat', [(order[p], order[(p + k) % n]) for p in range(n)])]
    pallas_call x6 -> x5, Pallas kernels: 34.9 us -> 30.1 us  [call(): pl.pallas_call(kernel, out_shape=out_shape, in_specs=[pl.BlockSpec(memory...]
    another operation x5 -> x0, other arithmetic: 4.73 us -> none  [the longest x4 4.11 us: apply(): return call(kernel, jnp.stack(rows), operands, specs, shape, m, blocks, [])]
  transfers between devices with their start and end apart: 15 -> 15, of which waited for: 7 -> 7; matrix products, arithmetic and copies ran while one was open for 7% -> 0% of each run, Pallas kernels for 33% -> 31%
where the time goes in v1:
time: 81.5 us; the launch traced here: 81.3 us
  waiting for transfers between devices  31.7 us (39%)
  Pallas kernels  30.1 us (37%)
  starting transfers between devices  18.6 us (23%)
    pallas_call x5, Pallas kernels, call(): pl.pallas_call(kernel, out_shape=out_shape, in_specs=[pl.BlockSpec(memory...  30.1 us
    ppermute x10, waiting for transfers between devices, turn(): lax.ppermute(x, 'feat', [(order[p], order[(p + k) % n]) for p in range(n)])  24.9 us
    ppermute x10, starting transfers between devices, turn(): lax.ppermute(x, 'feat', [(order[p], order[(p + k) % n]) for p in range(n)])  11.1 us
    ppermute x3, starting transfers between devices, scatter_sum(): lax.ppermute(y, 'feat', [(i, (i + 2 * k) % n) for i in range(n)])  5.73 us
    ppermute x1, waiting for transfers between devices, scatter_sum(): s = mine + lax.ppermute(theirs, 'feat', [(i, i ^ 1) for i in range(n)])  4.01 us
    ppermute x3, waiting for transfers between devices, scatter_sum(): lax.ppermute(y, 'feat', [(i, (i + 2 * k) % n) for i in range(n)])  2.75 us
    ppermute x1, starting transfers between devices, scatter_sum(): s = mine + lax.ppermute(theirs, 'feat', [(i, i ^ 1) for i in range(n)])  1.72 us
  transfers between devices with their start and end apart: 15, of which 7 were waited for; matrix products, arithmetic and copies ran while one was open for 0% of the time, Pallas kernels for 31%

profile of v1, /device:TPU:0, one launch (start us, length us, event | category | flops | bytes accessed | tf_op | source)
XLA Modules:
  0.0 81.3 jit_solution(12376048785763920829)
XLA Ops:
  0.0 3.1 %collective-permute-start = (bf16[128,2048]{1,0:T(8,128)(2,1)}, bf16[128,2048]{1,0:T(8,128)(2,1)}, u32[]{:S(2)}, u32[]{:S(2)}) collective-permute-start(bf16[128,2048]{1,0:T(8,128)(2,1)} %refs_0_.1), channel_id=1, source_target_pairs={{0,4},{4,8},{8,12},{12,14},{14,10},{10,6},{6,2},{2,0},{1,5},{5,9},... | collective-permute-start | bytes 1572872 | tf_op jit(solution)/shard_map/ppermute | solution.py:158
  3.1 0.0 collective-permute-start.4
  3.1 12.2 %collective-permute-done.refs_0_ = bf16[128,2048]{1,0:T(8,128)(2,1)} collective-permute-done((bf16[128,2048]{1,0:T(8,128)(2,1)}, bf16[128,2048]{1,0:T(8,128)(2,1)}, u32[]{:S(2)}, u32[]{:S(2)}) %collective-permute-start) | collective-permute-done | bytes 524320 | tf_op jit(solution)/shard_map/ppermute | solution.py:158
  15.3 1.8 %collective-permute-start.1 = (bf16[128,2048]{1,0:T(8,128)(2,1)}, bf16[128,2048]{1,0:T(8,128)(2,1)S(1)}, u32[]{:S(2)}, u32[]{:S(2)}) collective-permute-start(bf16[128,2048]{1,0:T(8,128)(2,1)} %collective-permute-done.refs_0_), channel_id=1, source_target_pairs={{0,4},{4,8},{8,12},{12,14},{14,10},{10,6},{6,2},{2,0},{1,5},{5,9},... | collective-permute-start | bytes 1572872 | tf_op jit(solution)/shard_map/ppermute | solution.py:158
  17.0 0.0 collective-permute-start.10
  17.0 0.0 collective-permute-done.4.refs_1_
  17.0 0.3 collective-permute-start.5
  17.3 11.3 %collective-permute-done.1.refs_0_ = bf16[128,2048]{1,0:T(8,128)(2,1)S(1)} collective-permute-done((bf16[128,2048]{1,0:T(8,128)(2,1)}, bf16[128,2048]{1,0:T(8,128)(2,1)S(1)}, u32[]{:S(2)}, u32[]{:S(2)}) %collective-permute-start.1) | collective-permute-done | bytes 524320 | tf_op jit(solution)/shard_map/ppermute | solution.py:158
  28.6 1.5 %collective-permute-start.2 = (bf16[128,1024]{1,0:T(8,128)(2,1)S(1)}, bf16[128,1024]{1,0:T(8,128)(2,1)S(1)}, u32[]{:S(2)}, u32[]{:S(2)}) collective-permute-start(bf16[128,1024]{1,0:T(8,128)(2,1)S(1)} %get-tuple-element.8), channel_id=1, source_target_pairs={{0,4},{4,8},{8,12},{12,14},{14,10},{10,6},{6,2},{2,0},{1,5},{5,9},... | collective-permute-start | bytes 786440 | tf_op jit(solution)/shard_map/ppermute | solution.py:158
  30.1 1.4 %collective-permute-done.5.refs_1_ = bf16[128,2048]{1,0:T(8,128)(2,1)S(1)} collective-permute-done((bf16[128,2048]{1,0:T(8,128)(2,1)}, bf16[128,2048]{1,0:T(8,128)(2,1)S(1)}, u32[]{:S(2)}, u32[]{:S(2)}) %collective-permute-start.5) | collective-permute-done | bytes 524320 | tf_op jit(solution)/shard_map/ppermute | solution.py:158
  31.6 0.3 collective-permute-start.6
  32.0 4.0 %shard_map.37.refs_3_ = f32[128,2048]{1,0:T(8,128)S(1)} custom-call(bf16[128,2048]{1,0:T(8,128)(2,1)S(1)} %copy-done.1, bf16[16384,2048]{1,0:T(8,128)(2,1)} %refs_2_.5), custom_call_target="tpu_custom_call" | custom-call | flops 1073741824 | bytes 8388608 | tf_op jit(solution)/shard_map/pallas_call | solution.py:103
  36.0 1.8 %collective-permute-start.8 = (bf16[128,1024]{1,0:T(8,128)(2,1)S(1)}, bf16[128,1024]{1,0:T(8,128)(2,1)S(1)}, u32[]{:S(2)}, u32[]{:S(2)}) collective-permute-start(bf16[128,1024]{1,0:T(8,128)(2,1)S(1)} %get-tuple-element.7), channel_id=1, source_target_pairs={{0,4},{4,8},{8,12},{12,14},{14,10},{10,6},{6,2},{2,0},{1,5},{5,9},... | collective-permute-start | bytes 786440 | tf_op jit(solution)/shard_map/ppermute | solution.py:158
  37.8 0.3 collective-permute-start.9
  38.0 7.8 %shard_map.38.refs_3_ = f32[128,2048]{1,0:T(8,128)S(1)} custom-call(bf16[128,2048]{1,0:T(8,128)(2,1)} %collective-permute-done.refs_0_, bf16[128,2048]{1,0:T(8,128)(2,1)} %collective-permute-done.4.refs_1_, bf16[16384,2048]{1,0:T(8,128)(2,1)} %refs_2_.5, f32[128,2048]{1,0:T(8,128)S(1)} %shard_map.37.refs_3_), custom_call_target="tpu_custom_call", output_to_operand_aliasing={{}: (3, {})} | custom-call | flops 2147483648 | bytes 16777216 | tf_op jit(solution)/shard_map/pallas_call | solution.py:103
  45.9 0.0 collective-permute-done.2.refs_0_
  45.9 1.8 %collective-permute-start.3 = (bf16[128,1024]{1,0:T(8,128)(2,1)S(1)}, bf16[128,1024]{1,0:T(8,128)(2,1)S(1)}, u32[]{:S(2)}, u32[]{:S(2)}) collective-permute-start(bf16[128,1024]{1,0:T(8,128)(2,1)S(1)} %collective-permute-done.2.refs_0_), channel_id=1, source_target_pairs={{0,4},{4,8},{8,12},{12,14},{14,10},{10,6},{6,2},{2,0},{1,5},{5,9},... | collective-permute-start | bytes 786440 | tf_op jit(solution)/shard_map/ppermute | solution.py:158
  47.7 0.3 collective-permute-start.7
  47.9 6.6 %shard_map.39.refs_5_ = f32[128,2048]{1,0:T(8,128)S(1)} custom-call(bf16[128,2048]{1,0:T(8,128)(2,1)S(1)} %collective-permute-done.1.refs_0_, bf16[128,2048]{1,0:T(8,128)(2,1)S(1)} %collective-permute-done.5.refs_1_, bf16[16384,2048]{1,0:T(8,128)(2,1)} %refs_2_.5, f32[128,2048]{1,0:T(8,128)S(1)} %shard_map.38.refs_3_), custom_call_target="tpu_custom_call", output_to_operand_aliasing={{}: (3, {})} | custom-call | flops 2147483648 | bytes 16777216 | tf_op jit(solution)/shard_map/pallas_call | solution.py:103
  54.6 0.0 copy-start
  54.6 0.0 collective-permute-done.9.refs_3_
  54.6 6.7 %shard_map.40.refs_3_ = f32[128,2048]{1,0:T(8,128)S(1)} custom-call(bf16[128,1024]{1,0:T(8,128)(2,1)S(1)} %collective-permute-done.2.refs_0_, bf16[128,1024]{1,0:T(8,128)(2,1)S(1)} %collective-permute-done.6.refs_1_, bf16[128,1024]{1,0:T(8,128)(2,1)S(1)} %collective-permute-done.8.refs_2_, ...), custom_call_target="tpu_custom_call", output_to_operand_aliasing={{}: (5, {})} | custom-call | flops 2147483648 | bytes 16777216 | tf_op jit(solution)/shard_map/pallas_call | solution.py:103
  61.4 5.0 %shard_map.41 = f32[768,128]{1,0:T(8,128)S(1)} custom-call(bf16[128,1024]{1,0:T(8,128)(2,1)S(1)} %collective-permute-done.3.refs_0_, bf16[128,1024]{1,0:T(8,128)(2,1)S(1)} %collective-permute-done.7.refs_1_, bf16[16384,2048]{1,0:T(8,128)(2,1)} %refs_2_.5, f32[128,2048]{1,0:T(8,128)S(1)} %shard_map.40.refs_3_, bf16[384,2048]{1,0:T(8,128)(2,1)S(1)} %copy-done, ...), custom_call_target="tpu_custom_call" | custom-call | flops 1879048192 | bytes 8388608 | tf_op jit(solution)/shard_map/pallas_call | solution.py:103
  66.4 1.7 %collective-permute-start.11 = (f32[4,96,128]{2,1,0:T(8,128)S(1)}, f32[4,96,128]{2,1,0:T(8,128)S(1)}, u32[]{:S(2)}, u32[]{:S(2)}) collective-permute-start(f32[4,96,128]{2,1,0:T(8,128)S(1)} %dynamic-slice_bitcast_fusion), channel_id=1, source_target_pairs={{0,2},{2,0},{4,6},{6,4},{8,10},{10,8},{12,14},{14,12},{1,3},{3,1},... | collective-permute-start | bytes 589832 | tf_op jit(solution)/shard_map/ppermute | solution.py:143
  68.1 4.0 %collective-permute-done.11 = f32[4,96,128]{2,1,0:T(8,128)S(1)} collective-permute-done((f32[4,96,128]{2,1,0:T(8,128)S(1)}, f32[4,96,128]{2,1,0:T(8,128)S(1)}, u32[]{:S(2)}, u32[]{:S(2)}) %collective-permute-start.11) | collective-permute-done | bytes 196640 | tf_op jit(solution)/shard_map/ppermute | solution.py:143
  72.2 1.8 %collective-permute-start.12 = (f32[96,128]{1,0:T(8,128)S(1)}, f32[96,128]{1,0:T(8,128)S(1)}, u32[]{:S(2)}, u32[]{:S(2)}) collective-permute-start(f32[96,128]{1,0:T(8,128)S(1)} %get-tuple-element.9), channel_id=1, source_target_pairs={{0,4},{2,6},{4,8},{6,10},{8,12},{10,14},{12,0},{14,2},{1,5},{3,7},... | collective-permute-start | bytes 147464 | tf_op jit(solution)/shard_map/ppermute | solution.py:147
  74.0 2.6 %collective-permute-start.13 = (f32[96,128]{1,0:T(8,128)S(1)}, f32[96,128]{1,0:T(8,128)S(1)}, u32[]{:S(2)}, u32[]{:S(2)}) collective-permute-start(f32[96,128]{1,0:T(8,128)S(1)} %get-tuple-element.11), channel_id=1, source_target_pairs={{0,8},{2,10},{4,12},{6,14},{8,0},{10,2},{12,4},{14,6},{1,9},{3,11}... | collective-permute-start | bytes 147464 | tf_op jit(solution)/shard_map/ppermute | solution.py:147
  76.6 1.3 %collective-permute-start.14 = (f32[96,128]{1,0:T(8,128)S(1)}, f32[96,128]{1,0:T(8,128)S(1)}, u32[]{:S(2)}, u32[]{:S(2)}) collective-permute-start(f32[96,128]{1,0:T(8,128)S(1)} %get-tuple-element.10), channel_id=1, source_target_pairs={{0,12},{2,14},{4,0},{6,2},{8,4},{10,6},{12,8},{14,10},{1,13},{3,15... | collective-permute-start | bytes 147464 | tf_op jit(solution)/shard_map/ppermute | solution.py:147
  77.9 0.2 collective-permute-done.12
  78.2 0.8 %collective-permute-done.13 = f32[96,128]{1,0:T(8,128)S(1)} collective-permute-done((f32[96,128]{1,0:T(8,128)S(1)}, f32[96,128]{1,0:T(8,128)S(1)}, u32[]{:S(2)}, u32[]{:S(2)}) %collective-permute-start.13) | collective-permute-done | bytes 49184 | tf_op jit(solution)/shard_map/ppermute | solution.py:147
  79.0 1.7 %collective-permute-done.14 = f32[96,128]{1,0:T(8,128)S(1)} collective-permute-done((f32[96,128]{1,0:T(8,128)S(1)}, f32[96,128]{1,0:T(8,128)S(1)}, u32[]{:S(2)}, u32[]{:S(2)}) %collective-permute-start.14) | collective-permute-done | bytes 49184 | tf_op jit(solution)/shard_map/ppermute | solution.py:147
  80.7 0.6 fusion.1
  (13 shorter events, 0.2 us)
Async XLA Ops:
  0.0 32.0 %copy-start.1 = (bf16[128,2048]{1,0:T(8,128)(2,1)S(1)}, bf16[128,2048]{1,0:T(8,128)(2,1)}, u32[]{:S(2)}) copy-start(bf16[128,2048]{1,0:T(8,128)(2,1)} %refs_0_.1) | copy-start | bytes 1572868
  0.0 15.3 %collective-permute-start = (bf16[128,2048]{1,0:T(8,128)(2,1)}, bf16[128,2048]{1,0:T(8,128)(2,1)}, u32[]{:S(2)}, u32[]{:S(2)}) collective-permute-start(bf16[128,2048]{1,0:T(8,128)(2,1)} %refs_0_.1), channel_id=1, source_target_pairs={{0,4},{4,8},{8,12},{12,14},{14,10},{10,6},{6,2},{2,0},{1,5},{5,9},... | collective-permute-start | bytes 1572872 | tf_op jit(solution)/shard_map/ppermute | solution.py:158
  3.1 14.0 %collective-permute-start.4 = (bf16[128,2048]{1,0:T(8,128)(2,1)}, bf16[128,2048]{1,0:T(8,128)(2,1)}, u32[]{:S(2)}, u32[]{:S(2)}) collective-permute-start(bf16[128,2048]{1,0:T(8,128)(2,1)} %refs_0_.1), channel_id=1, source_target_pairs={{0,2},{4,0},{8,4},{12,8},{14,12},{10,14},{6,10},{2,6},{1,3},{5,1},... | collective-permute-start | bytes 1572872 | tf_op jit(solution)/shard_map/ppermute | solution.py:158
  15.3 13.3 %collective-permute-start.1 = (bf16[128,2048]{1,0:T(8,128)(2,1)}, bf16[128,2048]{1,0:T(8,128)(2,1)S(1)}, u32[]{:S(2)}, u32[]{:S(2)}) collective-permute-start(bf16[128,2048]{1,0:T(8,128)(2,1)} %collective-permute-done.refs_0_), channel_id=1, source_target_pairs={{0,4},{4,8},{8,12},{12,14},{14,10},{10,6},{6,2},{2,0},{1,5},{5,9},... | collective-permute-start | bytes 1572872 | tf_op jit(solution)/shard_map/ppermute | solution.py:158
  17.0 44.3 %collective-permute-start.10 = (bf16[384,2048]{1,0:T(8,128)(2,1)}, bf16[384,2048]{1,0:T(8,128)(2,1)S(1)}, u32[]{:S(2)}, u32[]{:S(2)}) collective-permute-start(bf16[384,2048]{1,0:T(8,128)(2,1)} %refs_4_.3), channel_id=1, source_target_pairs={{0,1},{1,0},{2,3},{3,2},{4,5},{5,4},{6,7},{7,6},{8,9},{9,8},{10,11... | collective-permute-start | bytes 4718600 | tf_op jit(solution)/shard_map/ppermute | solution.py:164
  17.0 14.5 %collective-permute-start.5 = (bf16[128,2048]{1,0:T(8,128)(2,1)}, bf16[128,2048]{1,0:T(8,128)(2,1)S(1)}, u32[]{:S(2)}, u32[]{:S(2)}) collective-permute-start(bf16[128,2048]{1,0:T(8,128)(2,1)} %collective-permute-done.4.refs_1_), channel_id=1, source_target_pairs={{0,2},{4,0},{8,4},{12,8},{14,12},{10,14},{6,10},{2,6},{1,3},{5,1},... | collective-permute-start | bytes 1572872 | tf_op jit(solution)/shard_map/ppermute | solution.py:158
  28.6 17.2 %collective-permute-start.2 = (bf16[128,1024]{1,0:T(8,128)(2,1)S(1)}, bf16[128,1024]{1,0:T(8,128)(2,1)S(1)}, u32[]{:S(2)}, u32[]{:S(2)}) collective-permute-start(bf16[128,1024]{1,0:T(8,128)(2,1)S(1)} %get-tuple-element.8), channel_id=1, source_target_pairs={{0,4},{4,8},{8,12},{12,14},{14,10},{10,6},{6,2},{2,0},{1,5},{5,9},... | collective-permute-start | bytes 786440 | tf_op jit(solution)/shard_map/ppermute | solution.py:158
  31.6 16.0 %collective-permute-start.6 = (bf16[128,1024]{1,0:T(8,128)(2,1)S(1)}, bf16[128,1024]{1,0:T(8,128)(2,1)S(1)}, u32[]{:S(2)}, u32[]{:S(2)}) collective-permute-start(bf16[128,1024]{1,0:T(8,128)(2,1)S(1)} %get-tuple-element.6), channel_id=1, source_target_pairs={{0,2},{4,0},{8,4},{12,8},{14,12},{10,14},{6,10},{2,6},{1,3},{5,1},... | collective-permute-start | bytes 786440 | tf_op jit(solution)/shard_map/ppermute | solution.py:158
  36.0 18.6 %collective-permute-start.8 = (bf16[128,1024]{1,0:T(8,128)(2,1)S(1)}, bf16[128,1024]{1,0:T(8,128)(2,1)S(1)}, u32[]{:S(2)}, u32[]{:S(2)}) collective-permute-start(bf16[128,1024]{1,0:T(8,128)(2,1)S(1)} %get-tuple-element.7), channel_id=1, source_target_pairs={{0,4},{4,8},{8,12},{12,14},{14,10},{10,6},{6,2},{2,0},{1,5},{5,9},... | collective-permute-start | bytes 786440 | tf_op jit(solution)/shard_map/ppermute | solution.py:158
  37.8 16.8 %collective-permute-start.9 = (bf16[128,1024]{1,0:T(8,128)(2,1)S(1)}, bf16[128,1024]{1,0:T(8,128)(2,1)S(1)}, u32[]{:S(2)}, u32[]{:S(2)}) collective-permute-start(bf16[128,1024]{1,0:T(8,128)(2,1)S(1)} %get-tuple-element.5), channel_id=1, source_target_pairs={{0,2},{4,0},{8,4},{12,8},{14,12},{10,14},{6,10},{2,6},{1,3},{5,1},... | collective-permute-start | bytes 786440 | tf_op jit(solution)/shard_map/ppermute | solution.py:158
  45.9 15.5 %collective-permute-start.3 = (bf16[128,1024]{1,0:T(8,128)(2,1)S(1)}, bf16[128,1024]{1,0:T(8,128)(2,1)S(1)}, u32[]{:S(2)}, u32[]{:S(2)}) collective-permute-start(bf16[128,1024]{1,0:T(8,128)(2,1)S(1)} %collective-permute-done.2.refs_0_), channel_id=1, source_target_pairs={{0,4},{4,8},{8,12},{12,14},{14,10},{10,6},{6,2},{2,0},{1,5},{5,9},... | collective-permute-start | bytes 786440 | tf_op jit(solution)/shard_map/ppermute | solution.py:158
  47.7 13.7 %collective-permute-start.7 = (bf16[128,1024]{1,0:T(8,128)(2,1)S(1)}, bf16[128,1024]{1,0:T(8,128)(2,1)S(1)}, u32[]{:S(2)}, u32[]{:S(2)}) collective-permute-start(bf16[128,1024]{1,0:T(8,128)(2,1)S(1)} %collective-permute-done.6.refs_1_), channel_id=1, source_target_pairs={{0,2},{4,0},{8,4},{12,8},{14,12},{10,14},{6,10},{2,6},{1,3},{5,1},... | collective-permute-start | bytes 786440 | tf_op jit(solution)/shard_map/ppermute | solution.py:158
  54.6 6.8 %copy-start = (bf16[384,2048]{1,0:T(8,128)(2,1)S(1)}, bf16[384,2048]{1,0:T(8,128)(2,1)}, u32[]{:S(2)}) copy-start(bf16[384,2048]{1,0:T(8,128)(2,1)} %refs_4_.3) | copy-start | bytes 4718596
  66.4 5.7 %collective-permute-start.11 = (f32[4,96,128]{2,1,0:T(8,128)S(1)}, f32[4,96,128]{2,1,0:T(8,128)S(1)}, u32[]{:S(2)}, u32[]{:S(2)}) collective-permute-start(f32[4,96,128]{2,1,0:T(8,128)S(1)} %dynamic-slice_bitcast_fusion), channel_id=1, source_target_pairs={{0,2},{2,0},{4,6},{6,4},{8,10},{10,8},{12,14},{14,12},{1,3},{3,1},... | collective-permute-start | bytes 589832 | tf_op jit(solution)/shard_map/ppermute | solution.py:143
  72.2 5.9 %collective-permute-start.12 = (f32[96,128]{1,0:T(8,128)S(1)}, f32[96,128]{1,0:T(8,128)S(1)}, u32[]{:S(2)}, u32[]{:S(2)}) collective-permute-start(f32[96,128]{1,0:T(8,128)S(1)} %get-tuple-element.9), channel_id=1, source_target_pairs={{0,4},{2,6},{4,8},{6,10},{8,12},{10,14},{12,0},{14,2},{1,5},{3,7},... | collective-permute-start | bytes 147464 | tf_op jit(solution)/shard_map/ppermute | solution.py:147
  74.0 5.0 %collective-permute-start.13 = (f32[96,128]{1,0:T(8,128)S(1)}, f32[96,128]{1,0:T(8,128)S(1)}, u32[]{:S(2)}, u32[]{:S(2)}) collective-permute-start(f32[96,128]{1,0:T(8,128)S(1)} %get-tuple-element.11), channel_id=1, source_target_pairs={{0,8},{2,10},{4,12},{6,14},{8,0},{10,2},{12,4},{14,6},{1,9},{3,11}... | collective-permute-start | bytes 147464 | tf_op jit(solution)/shard_map/ppermute | solution.py:147
  76.6 4.1 %collective-permute-start.14 = (f32[96,128]{1,0:T(8,128)S(1)}, f32[96,128]{1,0:T(8,128)S(1)}, u32[]{:S(2)}, u32[]{:S(2)}) collective-permute-start(f32[96,128]{1,0:T(8,128)S(1)} %get-tuple-element.10), channel_id=1, source_target_pairs={{0,12},{2,14},{4,0},{6,2},{8,4},{10,6},{12,8},{14,10},{1,13},{3,15... | collective-permute-start | bytes 147464 | tf_op jit(solution)/shard_map/ppermute | solution.py:147

commit v2 on v1

v2 whole, which is shorter than its diff:
```python
import functools

import jax
import jax.numpy as jnp
from jax import lax
from jax.experimental import pallas as pl
from jax.experimental.pallas import tpu as pltpu
from jax.sharding import PartitionSpec as P


F32 = jnp.float32
BF16 = jnp.bfloat16
SLOTS = 5
TILE_ROWS = 512


def dot(a, b):
    return jnp.dot(a, b, preferred_element_type=F32)


def dot_t(a, b):
    return lax.dot_general(a, b, (((1,), (1,)), ((), ())), preferred_element_type=F32)


def ring_order(n):
    return list(range(0, n, 2)) + list(range(n - 1, 0, -2))


def ring_owner(n, k):
    me = lax.axis_index("feat")
    place = jnp.where(lax.rem(me, 2) == 0, lax.div(me, 2), n - 1 - lax.div(me, 2))
    place = lax.rem(place + k, n)
    return jnp.where(place < n // 2, 2 * place, 2 * (n - 1 - place) + 1)


def stream(n, rows, blocks, loads, m_ref, tiles, sems, acc_refs):
    slots, depth, width = tiles.shape
    counts = [b[0].shape[1] // depth for b in blocks]
    total = sum(counts)
    core = lax.axis_index("corp")
    half = width // 2
    starts = [
        ring_owner(n, jnp.where(core == 0, k, n - k)) * width + (1 - core if flip else core) * half for k, flip in rows
    ]

    def copy(i, start):
        slot = lax.rem(i, slots)
        at = pl.ds(pl.multiple_of(start, depth), depth)
        return pltpu.make_async_copy(m_ref.at[at, :], tiles.at[slot], sems.at[slot])

    def start_of(i):
        row, base = starts[0] + i * depth, counts[0]
        for b in range(1, len(blocks)):
            row = jnp.where(i >= base, starts[b] + (i - base) * depth, row)
            base += counts[b]
        return row

    for i in range(min(slots, total)):
        copy(i, start_of(i)).start()
    first = 0
    for block, count in zip(blocks, counts):
        for load in loads[: len(block)]:
            load.wait()
        loads = loads[len(block) :]

        def step(j, carry, block=block, first=first):
            i = first + j
            copy(i, 0).wait()
            at = pl.ds(pl.multiple_of(j * depth, depth), depth)
            piece = jnp.concatenate([ref[:, at] for ref in block], 0)
            product = dot(piece, tiles[lax.rem(i, slots)])
            docs = block[0].shape[0]
            for k, acc_ref in enumerate(acc_refs):
                acc_ref[...] += product[k * docs : (k + 1) * docs]

            @pl.when(i + slots < total)
            def _():
                copy(i + slots, start_of(i + slots)).start()

            return carry

        lax.fori_loop(0, count, step, 0)
        first += count


def apply_kernel(n, rows, sets, has_acc, *refs):
    count = sets * len(rows)
    m_ref, out_refs, (pieces, piece_sems, tiles, sems) = refs[count], refs[-4 - sets : -4], refs[-4:]
    loads = [pltpu.make_async_copy(refs[i], pieces.at[i], piece_sems.at[i]) for i in range(count)]
    for load in loads:
        load.start()
    if not has_acc:
        for out_ref in out_refs:
            out_ref[...] = jnp.zeros_like(out_ref)
    blocks = [[pieces.at[b * sets + k] for k in range(sets)] for b in range(len(rows))]
    stream(n, rows, blocks, loads, m_ref, tiles, sems, out_refs)


def apply(n, accs, blocks, rows, m):
    pieces = [p for b in blocks for p in b]
    sets = len(blocks[0])
    docs, span = pieces[0].shape
    depth = min(TILE_ROWS, span)
    any_spec = pl.BlockSpec(memory_space=pl.ANY)
    vmem = pl.BlockSpec(memory_space=pltpu.VMEM)
    return pl.pallas_call(
        functools.partial(apply_kernel, n, rows, sets, bool(accs)),
        out_shape=[jax.ShapeDtypeStruct((docs, m.shape[1]), F32)] * sets,
        in_specs=[any_spec] * (len(pieces) + 1) + [vmem] * len(accs),
        out_specs=[vmem] * sets,
        scratch_shapes=[
            pltpu.VMEM((len(pieces), docs, span), BF16),
            pltpu.SemaphoreType.DMA((len(pieces),)),
            pltpu.VMEM((SLOTS, depth, m.shape[1]), BF16),
            pltpu.SemaphoreType.DMA((SLOTS,)),
        ],
        input_output_aliases={len(pieces) + 1 + k: k for k in range(len(accs))},
        cost_estimate=pl.CostEstimate(
            flops=2 * docs * len(pieces) * span * m.shape[1],
            bytes_accessed=2 * len(blocks) * span * m.shape[1],
            transcendentals=0,
        ),
        compiler_params=pltpu.CompilerParams(vmem_limit_bytes=24 << 20),
    )(*pieces, m, *accs)


def score_kernel(*refs):
    first_ref, second_ref, *q_refs, out_ref, pair = refs
    docs = first_ref.shape[0]
    total = first_ref[...] + second_ref[...]
    hi = total.astype(BF16)
    pair[:docs, :] = hi
    pair[docs:, :] = (total - hi.astype(F32)).astype(BF16)
    height = q_refs[0].shape[0]
    for k, q_ref in enumerate(q_refs):
        place = lax.rem(lax.axis_index("corp") + len(q_refs) - k, len(q_refs))
        both = dot_t(q_ref[...], pair[...])
        out_ref[pl.ds(pl.multiple_of(place * height, height), height), :] = both[:, :docs] + both[:, docs:]


def score(first, second, parts):
    queries = sum(p.shape[0] for p in parts)
    docs, width = first.shape
    vmem = pl.BlockSpec(memory_space=pltpu.VMEM)
    return pl.pallas_call(
        score_kernel,
        out_shape=jax.ShapeDtypeStruct((queries, docs), F32),
        in_specs=[vmem] * (2 + len(parts)),
        out_specs=vmem,
        scratch_shapes=[pltpu.VMEM((2 * docs, width), BF16)],
        cost_estimate=pl.CostEstimate(
            flops=4 * queries * docs * width, bytes_accessed=2 * queries * width, transcendentals=0
        ),
        compiler_params=pltpu.CompilerParams(vmem_limit_bytes=16 << 20),
    )(first, second, *parts)


def scatter_sum(s, n):
    me = lax.axis_index("feat")
    x, z, m = lax.rem(me, 2), lax.div(me, 2), n // 2
    s = s.reshape((m, 2) + s.shape[1:])
    mine = lax.dynamic_index_in_dim(s, x, 1, False)
    theirs = lax.dynamic_index_in_dim(s, 1 - x, 1, False)
    s = mine + lax.ppermute(theirs, "feat", [(i, i ^ 1) for i in range(n)])
    out = lax.dynamic_index_in_dim(s, z, 0, False)
    for k in range(1, m):
        y = lax.dynamic_index_in_dim(s, lax.rem(z + k, m), 0, False)
        out = out + lax.ppermute(y, "feat", [(i, (i + 2 * k) % n) for i in range(n)])
    return out


def ring_body(n, q, m, d):
    docs, width = d.shape
    half = width // 2
    far = n // 2
    order = ring_order(n)
    core = lax.axis_index("corp")

    def move(x, shift, cross):
        pairs = [
            (2 * order[p] + c, 2 * order[(p + shift(c)) % n] + (c ^ cross)) for p in range(n) for c in range(2)
        ]
        return lax.ppermute(x, ("feat", "corp"), pairs)

    def fore(c):
        return 1 - 2 * c

    def back(c):
        return 2 * c - 1

    p_fore = p_back = lax.dynamic_slice(d, (0, core * half), (docs, half))
    r_fore = r_back = lax.dynamic_slice(d, (0, (1 - core) * half), (docs, half))
    own_p = p_fore
    own_r = move(r_fore, lambda c: 0, 1)
    parts = [q, lax.ppermute(q, "corp", [(0, 1), (1, 0)])]
    accs = []
    blocks, rows = [(own_p, own_r)], [(0, False)]
    for s in range(1, far):
        r_ways = (back, fore) if s == 1 else (fore, back)
        p_fore, p_back = move(p_fore, fore, 0), move(p_back, back, 0)
        r_fore = move(r_fore, r_ways[0], s == 1)
        r_back = move(r_back, r_ways[1], s == 1)
        accs = apply(n, accs, blocks, rows, m)
        blocks, rows = [(p_fore, r_fore), (p_back, r_back)], [(n - s, False), (s, False)]

    z_p, z_r = move(p_fore, fore, 0), move(r_fore, fore, 1)
    mine, theirs = apply(n, accs, blocks, rows, m)
    other = lax.ppermute(theirs, "corp", [(0, 1), (1, 0)])
    (mine,) = apply(n, [mine], [(z_p,), (z_r,)], [(far, False), (far, True)], m)
    scores = score(mine, other, parts)
    return scatter_sum(scores.reshape(n, -1, docs), n)


def plain_body(q, m, d):
    applied = dot(lax.all_gather(d, "feat", axis=1, tiled=True), m)
    left = lax.all_gather(q, "corp", axis=0, tiled=True).astype(F32)
    scores = lax.dot_general(
        left, applied, (((1,), (1,)), ((), ())), precision=lax.Precision.HIGHEST, preferred_element_type=F32
    )
    return lax.psum_scatter(scores, "feat", scatter_dimension=0, tiled=True)


def solution(mesh):
    n, n_corp = mesh.shape["feat"], mesh.shape["corp"]
    ring = n % 4 == 0 and 8 <= n <= 16 and n_corp == 2

    def on_device(q, m, d):
        if not ring:
            return plain_body(q, m, d)
        return ring_body(n, q, m, d)

    placed = (P(("groups", "corp"), "feat"), P(None, "feat"), P(("groups", "corp"), "feat"))
    return jax.shard_map(
        on_device,
        mesh=mesh,
        in_specs=placed,
        out_specs=P(("groups", "feat"), "corp"),
        check_vma=False,
    )
```

time: 81.5 us -> 78.1 us (0.958)
  starting transfers between devices: 18.6 us -> 31.9 us
  waiting for transfers between devices: 31.7 us -> 20.2 us
  Pallas kernels: 30.1 us -> 23.8 us
  local copies, waits for them, and re-layouts: 0.12 us -> 1.11 us
    ppermute x11 -> x17, starting transfers between devices: 11.1 us -> 25.1 us  [the longest x15 23.3 us: move(): return lax.ppermute(x, ('feat', 'corp'), pairs)]
    ppermute x11 -> x17, waiting for transfers between devices: 24.9 us -> 11.2 us  [the longest x15 11.2 us: move(): return lax.ppermute(x, ('feat', 'corp'), pairs)]
    pallas_call x5 -> x6, Pallas kernels: 30.1 us -> 23.8 us  [the longest x5 21.4 us: apply(): pl.pallas_call(functools.partial(apply_kernel, n, rows, sets, bool(accs))...]
    ppermute x1, waiting for transfers between devices: 4.01 us -> 6.69 us  [scatter_sum(): s = mine + lax.ppermute(theirs, 'feat', [(i, i ^ 1) for i in range(n)])]
    ppermute x1, starting transfers between devices: 1.72 us -> 0.07 us  [scatter_sum(): s = mine + lax.ppermute(theirs, 'feat', [(i, i ^ 1) for i in range(n)])]
    dynamic_slice x0 -> x1, local copies, waits for them, and re-layouts: none -> 1.06 us  [ring_body(): r_fore = r_back = lax.dynamic_slice(d, (0, (1 - core) * half), (docs, half))]
    ppermute x3, starting transfers between devices: 5.73 us -> 6.73 us  [scatter_sum(): lax.ppermute(y, 'feat', [(i, (i + 2 * k) % n) for i in range(n)])]
  transfers between devices with their start and end apart: 15 -> 21, of which waited for: 7 -> 7; matrix products, arithmetic and copies ran while one was open for 0% -> 0% of each run, Pallas kernels for 31% -> 27%
where the time goes in v2:
time: 78.1 us; the launch traced here: 78 us
  starting transfers between devices  31.9 us (41%)
  Pallas kernels  23.8 us (30%)
  waiting for transfers between devices  20.2 us (26%)
  local copies, waits for them, and re-layouts  1.11 us (1%)
    ppermute x15, starting transfers between devices, move(): return lax.ppermute(x, ('feat', 'corp'), pairs)  23.3 us
    pallas_call x5, Pallas kernels, apply(): pl.pallas_call(functools.partial(apply_kernel, n, rows, sets, bool(accs))...  21.4 us
    ppermute x15, waiting for transfers between devices, move(): return lax.ppermute(x, ('feat', 'corp'), pairs)  11.2 us
    ppermute x3, starting transfers between devices, scatter_sum(): lax.ppermute(y, 'feat', [(i, (i + 2 * k) % n) for i in range(n)])  6.73 us
    ppermute x1, waiting for transfers between devices, scatter_sum(): s = mine + lax.ppermute(theirs, 'feat', [(i, i ^ 1) for i in range(n)])  6.69 us
    pallas_call x1, Pallas kernels, score(): pl.pallas_call(score_kernel, out_shape=jax.ShapeDtypeStruct((queries, doc...  2.42 us
    ppermute x3, waiting for transfers between devices, scatter_sum(): lax.ppermute(y, 'feat', [(i, (i + 2 * k) % n) for i in range(n)])  2.39 us
    ppermute x1, starting transfers between devices, ring_body(): other = lax.ppermute(theirs, 'corp', [(0, 1), (1, 0)])  1.8 us
  transfers between devices with their start and end apart: 21, of which 7 were waited for; matrix products, arithmetic and copies ran while one was open for 0% of the time, Pallas kernels for 27%

profile of v2, /device:TPU:0, one launch (start us, length us, event | category | flops | bytes accessed | tf_op | source)
XLA Modules:
  0.0 78.0 jit_solution(6381253480286790774)
XLA Ops:
  0.0 1.1 %constant_dynamic-slice_fusion = (bf16[128,1024]{1,0:T(8,128)(2,1)S(1)}, bf16[128,1024]{1,0:T(8,128)(2,1)S(1)}) fusion(bf16[128,2048]{1,0:T(8,128)(2,1)} %param.5, s32[]{:T(128)S(6)} %select_n.27, s32[]{:T(128)S(6)} %select_n.26), kind=kLoop, calls=%fused_computation.8 | loop fusion | bytes 1048584 | tf_op jit(solution)/shard_map/dynamic_slice | solution.py:192
  1.1 3.1 %collective-permute-start = (bf16[128,1024]{1,0:T(8,128)(2,1)S(1)}, bf16[128,1024]{1,0:T(8,128)(2,1)S(1)}, u32[]{:S(2)}, u32[]{:S(2)}) collective-permute-start(bf16[128,1024]{1,0:T(8,128)(2,1)S(1)} %get-tuple-element.22.refs_0_), channel_id=1, source_target_pairs={{0,4},{1,3},{4,8},{5,1},{8,12},{9,5},{12,14},{13,9},{14,10},{15,13... | collective-permute-start | bytes 786440 | tf_op jit(solution)/shard_map/ppermute | solution.py:183
  4.2 0.7 collective-permute-start.4
  4.8 1.6 %collective-permute-start.8 = (bf16[128,1024]{1,0:T(8,128)(2,1)S(1)}, bf16[128,1024]{1,0:T(8,128)(2,1)S(1)}, u32[]{:S(2)}, u32[]{:S(2)}) collective-permute-start(bf16[128,1024]{1,0:T(8,128)(2,1)S(1)} %get-tuple-element.22.refs_0_), channel_id=1, source_target_pairs={{0,2},{1,5},{4,0},{5,9},{8,4},{9,13},{12,8},{13,15},{14,12},{15,11... | collective-permute-start | bytes 786440 | tf_op jit(solution)/shard_map/ppermute | solution.py:183
  6.4 1.9 %collective-permute-start.11 = (bf16[128,1024]{1,0:T(8,128)(2,1)S(1)}, bf16[128,1024]{1,0:T(8,128)(2,1)S(1)}, u32[]{:S(2)}, u32[]{:S(2)}) collective-permute-start(bf16[128,1024]{1,0:T(8,128)(2,1)S(1)} %get-tuple-element.21), channel_id=1, source_target_pairs={{0,5},{1,2},{4,9},{5,0},{8,13},{9,4},{12,15},{13,8},{14,11},{15,12... | collective-permute-start | bytes 786440 | tf_op jit(solution)/shard_map/ppermute | solution.py:183
  8.3 1.6 %collective-permute-done.refs_0_ = bf16[128,1024]{1,0:T(8,128)(2,1)S(1)} collective-permute-done((bf16[128,1024]{1,0:T(8,128)(2,1)S(1)}, bf16[128,1024]{1,0:T(8,128)(2,1)S(1)}, u32[]{:S(2)}, u32[]{:S(2)}) %collective-permute-start) | collective-permute-done | bytes 262176 | tf_op jit(solution)/shard_map/ppermute | solution.py:183
  9.9 2.5 %collective-permute-start.1 = (bf16[128,1024]{1,0:T(8,128)(2,1)S(1)}, bf16[128,1024]{1,0:T(8,128)(2,1)S(1)}, u32[]{:S(2)}, u32[]{:S(2)}) collective-permute-start(bf16[128,1024]{1,0:T(8,128)(2,1)S(1)} %collective-permute-done.refs_0_), channel_id=1, source_target_pairs={{0,4},{1,3},{4,8},{5,1},{8,12},{9,5},{12,14},{13,9},{14,10},{15,13... | collective-permute-start | bytes 786440 | tf_op jit(solution)/shard_map/ppermute | solution.py:183
  12.4 2.0 %collective-permute-start.5 = (bf16[128,1024]{1,0:T(8,128)(2,1)S(1)}, bf16[128,1024]{1,0:T(8,128)(2,1)S(1)}, u32[]{:S(2)}, u32[]{:S(2)}) collective-permute-start(bf16[128,1024]{1,0:T(8,128)(2,1)S(1)} %collective-permute-done.4.refs_1_), channel_id=1, source_target_pairs={{0,4},{1,3},{4,8},{5,1},{8,12},{9,5},{12,14},{13,9},{14,10},{15,13... | collective-permute-start | bytes 786440 | tf_op jit(solution)/shard_map/ppermute | solution.py:183
  14.4 2.7 %collective-permute-done.8.refs_2_ = bf16[128,1024]{1,0:T(8,128)(2,1)S(1)} collective-permute-done((bf16[128,1024]{1,0:T(8,128)(2,1)S(1)}, bf16[128,1024]{1,0:T(8,128)(2,1)S(1)}, u32[]{:S(2)}, u32[]{:S(2)}) %collective-permute-start.8) | collective-permute-done | bytes 262176 | tf_op jit(solution)/shard_map/ppermute | solution.py:183
  17.1 1.8 %collective-permute-start.9 = (bf16[128,1024]{1,0:T(8,128)(2,1)S(1)}, bf16[128,1024]{1,0:T(8,128)(2,1)S(1)}, u32[]{:S(2)}, u32[]{:S(2)}) collective-permute-start(bf16[128,1024]{1,0:T(8,128)(2,1)S(1)} %collective-permute-done.8.refs_2_), channel_id=1, source_target_pairs={{0,2},{1,5},{4,0},{5,9},{8,4},{9,13},{12,8},{13,15},{14,12},{15,11... | collective-permute-start | bytes 786440 | tf_op jit(solution)/shard_map/ppermute | solution.py:183
  18.9 2.3 %collective-permute-start.12 = (bf16[128,1024]{1,0:T(8,128)(2,1)S(1)}, bf16[128,1024]{1,0:T(8,128)(2,1)S(1)}, u32[]{:S(2)}, u32[]{:S(2)}) collective-permute-start(bf16[128,1024]{1,0:T(8,128)(2,1)S(1)} %collective-permute-done.11.refs_3_), channel_id=1, source_target_pairs={{0,2},{1,5},{4,0},{5,9},{8,4},{9,13},{12,8},{13,15},{14,12},{15,11... | collective-permute-start | bytes 786440 | tf_op jit(solution)/shard_map/ppermute | solution.py:183
  21.2 3.1 %shard_map.37 = (f32[128,2048]{1,0:T(8,128)S(1)}, f32[128,2048]{1,0:T(8,128)S(1)}) custom-call(bf16[128,1024]{1,0:T(8,128)(2,1)S(1)} %get-tuple-element.22.refs_0_, bf16[128,1024]{1,0:T(8,128)(2,1)S(1)} %collective-permute-done.14.refs_1_, bf16[16384,2048]{1,0:T(8,128)(2,1)} %refs_2_.4), custom_call_target="tpu_custom_call" | custom-call | flops 1073741824 | bytes 4194304 | tf_op jit(solution)/shard_map/pallas_call | solution.py:106
  24.4 1.4 %collective-permute-start.2 = (bf16[128,1024]{1,0:T(8,128)(2,1)S(1)}, bf16[128,1024]{1,0:T(8,128)(2,1)S(1)}, u32[]{:S(2)}, u32[]{:S(2)}) collective-permute-start(bf16[128,1024]{1,0:T(8,128)(2,1)S(1)} %collective-permute-done.1.refs_0_), channel_id=1, source_target_pairs={{0,4},{1,3},{4,8},{5,1},{8,12},{9,5},{12,14},{13,9},{14,10},{15,13... | collective-permute-start | bytes 786440 | tf_op jit(solution)/shard_map/ppermute | solution.py:183
  25.8 0.7 collective-permute-start.6
  26.5 1.3 %collective-permute-start.10 = (bf16[128,1024]{1,0:T(8,128)(2,1)S(1)}, bf16[128,1024]{1,0:T(8,128)(2,1)S(1)}, u32[]{:S(2)}, u32[]{:S(2)}) collective-permute-start(bf16[128,1024]{1,0:T(8,128)(2,1)S(1)} %collective-permute-done.9.refs_2_), channel_id=1, source_target_pairs={{0,2},{1,5},{4,0},{5,9},{8,4},{9,13},{12,8},{13,15},{14,12},{15,11... | collective-permute-start | bytes 786440 | tf_op jit(solution)/shard_map/ppermute | solution.py:183
  27.9 1.6 %collective-permute-start.13 = (bf16[128,1024]{1,0:T(8,128)(2,1)S(1)}, bf16[128,1024]{1,0:T(8,128)(2,1)S(1)}, u32[]{:S(2)}, u32[]{:S(2)}) collective-permute-start(bf16[128,1024]{1,0:T(8,128)(2,1)S(1)} %collective-permute-done.12.refs_3_), channel_id=1, source_target_pairs={{0,2},{1,5},{4,0},{5,9},{8,4},{9,13},{12,8},{13,15},{14,12},{15,11... | collective-permute-start | bytes 786440 | tf_op jit(solution)/shard_map/ppermute | solution.py:183
  29.4 4.7 %shard_map.38 = (f32[128,2048]{1,0:T(8,128)S(1)}, f32[128,2048]{1,0:T(8,128)S(1)}) custom-call(bf16[128,1024]{1,0:T(8,128)(2,1)S(1)} %collective-permute-done.refs_0_, bf16[128,1024]{1,0:T(8,128)(2,1)S(1)} %collective-permute-done.4.refs_1_, bf16[128,1024]{1,0:T(8,128)(2,1)S(1)} %collective-permute-done.8.refs_2_, ...), custom_call_target="tpu_custom_call", output_to_operand_aliasing={{0}: (5, {}), {1}: (6, {})} | custom-call | flops 2147483648 | bytes 8388608 | tf_op jit(solution)/shard_map/pallas_call | solution.py:106
  34.1 4.6 %shard_map.39 = (f32[128,2048]{1,0:T(8,128)S(1)}, f32[128,2048]{1,0:T(8,128)S(1)}) custom-call(bf16[128,1024]{1,0:T(8,128)(2,1)S(1)} %collective-permute-done.1.refs_0_, bf16[128,1024]{1,0:T(8,128)(2,1)S(1)} %collective-permute-done.5.refs_1_, bf16[128,1024]{1,0:T(8,128)(2,1)S(1)} %collective-permute-done.9.refs_2_, ...), custom_call_target="tpu_custom_call", output_to_operand_aliasing={{0}: (5, {}), {1}: (6, {})} | custom-call | flops 2147483648 | bytes 8388608 | tf_op jit(solution)/shard_map/pallas_call | solution.py:106
  38.8 4.7 %shard_map.40 = (f32[128,2048]{1,0:T(8,128)S(1)}, f32[128,2048]{1,0:T(8,128)S(1)}) custom-call(bf16[128,1024]{1,0:T(8,128)(2,1)S(1)} %collective-permute-done.2.refs_0_, bf16[128,1024]{1,0:T(8,128)(2,1)} %collective-permute-done.6.refs_1_, bf16[128,1024]{1,0:T(8,128)(2,1)S(1)} %collective-permute-done.10.refs_2_, ...), custom_call_target="tpu_custom_call", output_to_operand_aliasing={{0}: (5, {}), {1}: (6, {})} | custom-call | flops 2147483648 | bytes 8388608 | tf_op jit(solution)/shard_map/pallas_call | solution.py:106
  43.5 1.8 %collective-permute-start.15 = (f32[128,2048]{1,0:T(8,128)S(1)}, f32[128,2048]{1,0:T(8,128)S(1)}, u32[]{:S(2)}, u32[]{:S(2)}) collective-permute-start(f32[128,2048]{1,0:T(8,128)S(1)} %get-tuple-element.20), channel_id=1, source_target_pairs={{0,1},{1,0},{2,3},{3,2},{4,5},{5,4},{6,7},{7,6},{8,9},{9,8},{10,11... | collective-permute-start | bytes 3145736 | tf_op jit(solution)/shard_map/ppermute | solution.py:208
  45.3 2.5 %collective-permute-start.3 = (bf16[128,1024]{1,0:T(8,128)(2,1)S(1)}, bf16[128,1024]{1,0:T(8,128)(2,1)}, u32[]{:S(2)}, u32[]{:S(2)}) collective-permute-start(bf16[128,1024]{1,0:T(8,128)(2,1)S(1)} %collective-permute-done.2.refs_0_), channel_id=1, source_target_pairs={{0,4},{1,3},{4,8},{5,1},{8,12},{9,5},{12,14},{13,9},{14,10},{15,13... | collective-permute-start | bytes 786440 | tf_op jit(solution)/shard_map/ppermute | solution.py:183
  47.8 4.0 %collective-permute-done.3.refs_0_ = bf16[128,1024]{1,0:T(8,128)(2,1)} collective-permute-done((bf16[128,1024]{1,0:T(8,128)(2,1)S(1)}, bf16[128,1024]{1,0:T(8,128)(2,1)}, u32[]{:S(2)}, u32[]{:S(2)}) %collective-permute-start.3) | collective-permute-done | bytes 262176 | tf_op jit(solution)/shard_map/ppermute | solution.py:183
  51.8 2.8 %collective-permute-done.7.refs_1_ = bf16[128,1024]{1,0:T(8,128)(2,1)} collective-permute-done((bf16[128,1024]{1,0:T(8,128)(2,1)}, bf16[128,1024]{1,0:T(8,128)(2,1)}, u32[]{:S(2)}, u32[]{:S(2)}) %collective-permute-start.7) | collective-permute-done | bytes 262176 | tf_op jit(solution)/shard_map/ppermute | solution.py:183
  54.6 4.3 %shard_map.41.refs_0_ = f32[128,2048]{1,0:T(8,128)S(1)} custom-call(bf16[128,1024]{1,0:T(8,128)(2,1)} %collective-permute-done.3.refs_0_, bf16[128,1024]{1,0:T(8,128)(2,1)} %collective-permute-done.7.refs_1_, bf16[16384,2048]{1,0:T(8,128)(2,1)} %refs_2_.4, f32[128,2048]{1,0:T(8,128)S(1)} %get-tuple-element.19.refs_3_), custom_call_target="tpu_custom_call", output_to_operand_aliasing={{}: (3, {})} | custom-call | flops 1073741824 | bytes 8388608 | tf_op jit(solution)/shard_map/pallas_call | solution.py:106
  58.9 2.4 %shard_map.42 = f32[768,128]{1,0:T(8,128)S(1)} custom-call(f32[128,2048]{1,0:T(8,128)S(1)} %shard_map.41.refs_0_, f32[128,2048]{1,0:T(8,128)S(1)} %collective-permute-done.15.refs_1_, bf16[384,2048]{1,0:T(8,128)(2,1)S(1)} %copy-done, bf16[384,2048]{1,0:T(8,128)(2,1)} %collective-permute-done.16.refs_3_), custom_call_target="tpu_custom_call" | custom-call | flops 805306368 | bytes 3145728 | tf_op jit(solution)/shard_map/pallas_call | solution.py:145
  61.4 6.7 %collective-permute-done.17 = f32[4,96,128]{2,1,0:T(8,128)S(1)} collective-permute-done((f32[4,96,128]{2,1,0:T(8,128)S(1)}, f32[4,96,128]{2,1,0:T(8,128)S(1)}, u32[]{:S(2)}, u32[]{:S(2)}) %collective-permute-start.17) | collective-permute-done | bytes 196640 | tf_op jit(solution)/shard_map/ppermute | solution.py:164
  68.2 2.4 %collective-permute-start.18 = (f32[96,128]{1,0:T(8,128)S(1)}, f32[96,128]{1,0:T(8,128)S(1)}, u32[]{:S(2)}, u32[]{:S(2)}) collective-permute-start(f32[96,128]{1,0:T(8,128)S(1)} %get-tuple-element.23), channel_id=1, source_target_pairs={{0,4},{2,6},{4,8},{6,10},{8,12},{10,14},{12,0},{14,2},{1,5},{3,7},... | collective-permute-start | bytes 147464 | tf_op jit(solution)/shard_map/ppermute | solution.py:168
  70.6 2.6 %collective-permute-start.19 = (f32[96,128]{1,0:T(8,128)S(1)}, f32[96,128]{1,0:T(8,128)S(1)}, u32[]{:S(2)}, u32[]{:S(2)}) collective-permute-start(f32[96,128]{1,0:T(8,128)S(1)} %get-tuple-element.25), channel_id=1, source_target_pairs={{0,8},{2,10},{4,12},{6,14},{8,0},{10,2},{12,4},{14,6},{1,9},{3,11}... | collective-permute-start | bytes 147464 | tf_op jit(solution)/shard_map/ppermute | solution.py:168
  73.2 1.7 %collective-permute-start.20 = (f32[96,128]{1,0:T(8,128)S(1)}, f32[96,128]{1,0:T(8,128)S(1)}, u32[]{:S(2)}, u32[]{:S(2)}) collective-permute-start(f32[96,128]{1,0:T(8,128)S(1)} %get-tuple-element.24), channel_id=1, source_target_pairs={{0,12},{2,14},{4,0},{6,2},{8,4},{10,6},{12,8},{14,10},{1,13},{3,15... | collective-permute-start | bytes 147464 | tf_op jit(solution)/shard_map/ppermute | solution.py:168
  74.9 1.6 %collective-permute-done.19 = f32[96,128]{1,0:T(8,128)S(1)} collective-permute-done((f32[96,128]{1,0:T(8,128)S(1)}, f32[96,128]{1,0:T(8,128)S(1)}, u32[]{:S(2)}, u32[]{:S(2)}) %collective-permute-start.19) | collective-permute-done | bytes 49184 | tf_op jit(solution)/shard_map/ppermute | solution.py:168
  76.6 0.8 collective-permute-done.20
  77.3 0.6 fusion.1
  (23 shorter events, 0.2 us)
Async XLA Ops:
  1.1 8.8 %collective-permute-start = (bf16[128,1024]{1,0:T(8,128)(2,1)S(1)}, bf16[128,1024]{1,0:T(8,128)(2,1)S(1)}, u32[]{:S(2)}, u32[]{:S(2)}) collective-permute-start(bf16[128,1024]{1,0:T(8,128)(2,1)S(1)} %get-tuple-element.22.refs_0_), channel_id=1, source_target_pairs={{0,4},{1,3},{4,8},{5,1},{8,12},{9,5},{12,14},{13,9},{14,10},{15,13... | collective-permute-start | bytes 786440 | tf_op jit(solution)/shard_map/ppermute | solution.py:183
  4.2 8.2 %collective-permute-start.4 = (bf16[128,1024]{1,0:T(8,128)(2,1)S(1)}, bf16[128,1024]{1,0:T(8,128)(2,1)S(1)}, u32[]{:S(2)}, u32[]{:S(2)}) collective-permute-start(bf16[128,1024]{1,0:T(8,128)(2,1)S(1)} %get-tuple-element.21), channel_id=1, source_target_pairs={{0,3},{1,4},{4,1},{5,8},{8,5},{9,12},{12,9},{13,14},{14,13},{15,10... | collective-permute-start | bytes 786440 | tf_op jit(solution)/shard_map/ppermute | solution.py:183
  4.8 12.2 %collective-permute-start.8 = (bf16[128,1024]{1,0:T(8,128)(2,1)S(1)}, bf16[128,1024]{1,0:T(8,128)(2,1)S(1)}, u32[]{:S(2)}, u32[]{:S(2)}) collective-permute-start(bf16[128,1024]{1,0:T(8,128)(2,1)S(1)} %get-tuple-element.22.refs_0_), channel_id=1, source_target_pairs={{0,2},{1,5},{4,0},{5,9},{8,4},{9,13},{12,8},{13,15},{14,12},{15,11... | collective-permute-start | bytes 786440 | tf_op jit(solution)/shard_map/ppermute | solution.py:183
  6.4 12.5 %collective-permute-start.11 = (bf16[128,1024]{1,0:T(8,128)(2,1)S(1)}, bf16[128,1024]{1,0:T(8,128)(2,1)S(1)}, u32[]{:S(2)}, u32[]{:S(2)}) collective-permute-start(bf16[128,1024]{1,0:T(8,128)(2,1)S(1)} %get-tuple-element.21), channel_id=1, source_target_pairs={{0,5},{1,2},{4,9},{5,0},{8,13},{9,4},{12,15},{13,8},{14,11},{15,12... | collective-permute-start | bytes 786440 | tf_op jit(solution)/shard_map/ppermute | solution.py:183
  8.3 12.9 %collective-permute-start.14 = (bf16[128,1024]{1,0:T(8,128)(2,1)S(1)}, bf16[128,1024]{1,0:T(8,128)(2,1)S(1)}, u32[]{:S(2)}, u32[]{:S(2)}) collective-permute-start(bf16[128,1024]{1,0:T(8,128)(2,1)S(1)} %get-tuple-element.21), channel_id=1, source_target_pairs={{0,1},{1,0},{4,5},{5,4},{8,9},{9,8},{12,13},{13,12},{14,15},{15,14... | collective-permute-start | bytes 786440 | tf_op jit(solution)/shard_map/ppermute | solution.py:183
  9.9 14.5 %collective-permute-start.1 = (bf16[128,1024]{1,0:T(8,128)(2,1)S(1)}, bf16[128,1024]{1,0:T(8,128)(2,1)S(1)}, u32[]{:S(2)}, u32[]{:S(2)}) collective-permute-start(bf16[128,1024]{1,0:T(8,128)(2,1)S(1)} %collective-permute-done.refs_0_), channel_id=1, source_target_pairs={{0,4},{1,3},{4,8},{5,1},{8,12},{9,5},{12,14},{13,9},{14,10},{15,13... | collective-permute-start | bytes 786440 | tf_op jit(solution)/shard_map/ppermute | solution.py:183
  12.4 13.5 %collective-permute-start.5 = (bf16[128,1024]{1,0:T(8,128)(2,1)S(1)}, bf16[128,1024]{1,0:T(8,128)(2,1)S(1)}, u32[]{:S(2)}, u32[]{:S(2)}) collective-permute-start(bf16[128,1024]{1,0:T(8,128)(2,1)S(1)} %collective-permute-done.4.refs_1_), channel_id=1, source_target_pairs={{0,4},{1,3},{4,8},{5,1},{8,12},{9,5},{12,14},{13,9},{14,10},{15,13... | collective-permute-start | bytes 786440 | tf_op jit(solution)/shard_map/ppermute | solution.py:183
  17.1 9.4 %collective-permute-start.9 = (bf16[128,1024]{1,0:T(8,128)(2,1)S(1)}, bf16[128,1024]{1,0:T(8,128)(2,1)S(1)}, u32[]{:S(2)}, u32[]{:S(2)}) collective-permute-start(bf16[128,1024]{1,0:T(8,128)(2,1)S(1)} %collective-permute-done.8.refs_2_), channel_id=1, source_target_pairs={{0,2},{1,5},{4,0},{5,9},{8,4},{9,13},{12,8},{13,15},{14,12},{15,11... | collective-permute-start | bytes 786440 | tf_op jit(solution)/shard_map/ppermute | solution.py:183
  18.9 8.9 %collective-permute-start.12 = (bf16[128,1024]{1,0:T(8,128)(2,1)S(1)}, bf16[128,1024]{1,0:T(8,128)(2,1)S(1)}, u32[]{:S(2)}, u32[]{:S(2)}) collective-permute-start(bf16[128,1024]{1,0:T(8,128)(2,1)S(1)} %collective-permute-done.11.refs_3_), channel_id=1, source_target_pairs={{0,2},{1,5},{4,0},{5,9},{8,4},{9,13},{12,8},{13,15},{14,12},{15,11... | collective-permute-start | bytes 786440 | tf_op jit(solution)/shard_map/ppermute | solution.py:183
  21.2 37.6 %collective-permute-start.16 = (bf16[384,2048]{1,0:T(8,128)(2,1)}, bf16[384,2048]{1,0:T(8,128)(2,1)}, u32[]{:S(2)}, u32[]{:S(2)}) collective-permute-start(bf16[384,2048]{1,0:T(8,128)(2,1)} %refs_2_.5), channel_id=1, source_target_pairs={{0,1},{1,0},{2,3},{3,2},{4,5},{5,4},{6,7},{7,6},{8,9},{9,8},{10,11... | collective-permute-start | bytes 4718600 | tf_op jit(solution)/shard_map/ppermute | solution.py:195
  24.4 14.4 %collective-permute-start.2 = (bf16[128,1024]{1,0:T(8,128)(2,1)S(1)}, bf16[128,1024]{1,0:T(8,128)(2,1)S(1)}, u32[]{:S(2)}, u32[]{:S(2)}) collective-permute-start(bf16[128,1024]{1,0:T(8,128)(2,1)S(1)} %collective-permute-done.1.refs_0_), channel_id=1, source_target_pairs={{0,4},{1,3},{4,8},{5,1},{8,12},{9,5},{12,14},{13,9},{14,10},{15,13... | collective-permute-start | bytes 786440 | tf_op jit(solution)/shard_map/ppermute | solution.py:183
  25.8 13.0 %collective-permute-start.6 = (bf16[128,1024]{1,0:T(8,128)(2,1)S(1)}, bf16[128,1024]{1,0:T(8,128)(2,1)}, u32[]{:S(2)}, u32[]{:S(2)}) collective-permute-start(bf16[128,1024]{1,0:T(8,128)(2,1)S(1)} %collective-permute-done.5.refs_1_), channel_id=1, source_target_pairs={{0,4},{1,3},{4,8},{5,1},{8,12},{9,5},{12,14},{13,9},{14,10},{15,13... | collective-permute-start | bytes 786440 | tf_op jit(solution)/shard_map/ppermute | solution.py:183
  26.5 12.3 %collective-permute-start.10 = (bf16[128,1024]{1,0:T(8,128)(2,1)S(1)}, bf16[128,1024]{1,0:T(8,128)(2,1)S(1)}, u32[]{:S(2)}, u32[]{:S(2)}) collective-permute-start(bf16[128,1024]{1,0:T(8,128)(2,1)S(1)} %collective-permute-done.9.refs_2_), channel_id=1, source_target_pairs={{0,2},{1,5},{4,0},{5,9},{8,4},{9,13},{12,8},{13,15},{14,12},{15,11... | collective-permute-start | bytes 786440 | tf_op jit(solution)/shard_map/ppermute | solution.py:183
  27.9 10.9 %collective-permute-start.13 = (bf16[128,1024]{1,0:T(8,128)(2,1)S(1)}, bf16[128,1024]{1,0:T(8,128)(2,1)S(1)}, u32[]{:S(2)}, u32[]{:S(2)}) collective-permute-start(bf16[128,1024]{1,0:T(8,128)(2,1)S(1)} %collective-permute-done.12.refs_3_), channel_id=1, source_target_pairs={{0,2},{1,5},{4,0},{5,9},{8,4},{9,13},{12,8},{13,15},{14,12},{15,11... | collective-permute-start | bytes 786440 | tf_op jit(solution)/shard_map/ppermute | solution.py:183
  43.5 15.3 %collective-permute-start.15 = (f32[128,2048]{1,0:T(8,128)S(1)}, f32[128,2048]{1,0:T(8,128)S(1)}, u32[]{:S(2)}, u32[]{:S(2)}) collective-permute-start(f32[128,2048]{1,0:T(8,128)S(1)} %get-tuple-element.20), channel_id=1, source_target_pairs={{0,1},{1,0},{2,3},{3,2},{4,5},{5,4},{6,7},{7,6},{8,9},{9,8},{10,11... | collective-permute-start | bytes 3145736 | tf_op jit(solution)/shard_map/ppermute | solution.py:208
  45.3 6.5 %collective-permute-start.3 = (bf16[128,1024]{1,0:T(8,128)(2,1)S(1)}, bf16[128,1024]{1,0:T(8,128)(2,1)}, u32[]{:S(2)}, u32[]{:S(2)}) collective-permute-start(bf16[128,1024]{1,0:T(8,128)(2,1)S(1)} %collective-permute-done.2.refs_0_), channel_id=1, source_target_pairs={{0,4},{1,3},{4,8},{5,1},{8,12},{9,5},{12,14},{13,9},{14,10},{15,13... | collective-permute-start | bytes 786440 | tf_op jit(solution)/shard_map/ppermute | solution.py:183
  47.8 6.8 %collective-permute-start.7 = (bf16[128,1024]{1,0:T(8,128)(2,1)}, bf16[128,1024]{1,0:T(8,128)(2,1)}, u32[]{:S(2)}, u32[]{:S(2)}) collective-permute-start(bf16[128,1024]{1,0:T(8,128)(2,1)} %collective-permute-done.6.refs_1_), channel_id=1, source_target_pairs={{0,5},{1,2},{4,9},{5,0},{8,13},{9,4},{12,15},{13,8},{14,11},{15,12... | collective-permute-start | bytes 786440 | tf_op jit(solution)/shard_map/ppermute | solution.py:183
  54.6 4.3 %copy-start = (bf16[384,2048]{1,0:T(8,128)(2,1)S(1)}, bf16[384,2048]{1,0:T(8,128)(2,1)}, u32[]{:S(2)}) copy-start(bf16[384,2048]{1,0:T(8,128)(2,1)} %refs_2_.5) | copy-start | bytes 4718596
  61.3 6.8 %collective-permute-start.17 = (f32[4,96,128]{2,1,0:T(8,128)S(1)}, f32[4,96,128]{2,1,0:T(8,128)S(1)}, u32[]{:S(2)}, u32[]{:S(2)}) collective-permute-start(f32[4,96,128]{2,1,0:T(8,128)S(1)} %dynamic-slice_bitcast_fusion), channel_id=1, source_target_pairs={{0,2},{2,0},{4,6},{6,4},{8,10},{10,8},{12,14},{14,12},{1,3},{3,1},... | collective-permute-start | bytes 589832 | tf_op jit(solution)/shard_map/ppermute | solution.py:164
  68.2 6.7 %collective-permute-start.18 = (f32[96,128]{1,0:T(8,128)S(1)}, f32[96,128]{1,0:T(8,128)S(1)}, u32[]{:S(2)}, u32[]{:S(2)}) collective-permute-start(f32[96,128]{1,0:T(8,128)S(1)} %get-tuple-element.23), channel_id=1, source_target_pairs={{0,4},{2,6},{4,8},{6,10},{8,12},{10,14},{12,0},{14,2},{1,5},{3,7},... | collective-permute-start | bytes 147464 | tf_op jit(solution)/shard_map/ppermute | solution.py:168
  70.6 6.0 %collective-permute-start.19 = (f32[96,128]{1,0:T(8,128)S(1)}, f32[96,128]{1,0:T(8,128)S(1)}, u32[]{:S(2)}, u32[]{:S(2)}) collective-permute-start(f32[96,128]{1,0:T(8,128)S(1)} %get-tuple-element.25), channel_id=1, source_target_pairs={{0,8},{2,10},{4,12},{6,14},{8,0},{10,2},{12,4},{14,6},{1,9},{3,11}... | collective-permute-start | bytes 147464 | tf_op jit(solution)/shard_map/ppermute | solution.py:168
  73.2 4.1 %collective-permute-start.20 = (f32[96,128]{1,0:T(8,128)S(1)}, f32[96,128]{1,0:T(8,128)S(1)}, u32[]{:S(2)}, u32[]{:S(2)}) collective-permute-start(f32[96,128]{1,0:T(8,128)S(1)} %get-tuple-element.24), channel_id=1, source_target_pairs={{0,12},{2,14},{4,0},{6,2},{8,4},{10,6},{12,8},{14,10},{1,13},{3,15... | collective-permute-start | bytes 147464 | tf_op jit(solution)/shard_map/ppermute | solution.py:168

commit v3 on v2

v3 whole, which is shorter than its diff:
```python
import functools

import jax
import jax.numpy as jnp
from jax import lax
from jax.experimental import pallas as pl
from jax.experimental.pallas import tpu as pltpu
from jax.sharding import PartitionSpec as P


F32 = jnp.float32
BF16 = jnp.bfloat16
SLOTS = 5
TILE_ROWS = 512
KEPT_ROWS = 1024


def dot(a, b):
    return jnp.dot(a, b, preferred_element_type=F32)


def dot_t(a, b):
    return lax.dot_general(a, b, (((1,), (1,)), ((), ())), preferred_element_type=F32)


def ring_order(n):
    return list(range(0, n, 2)) + list(range(n - 1, 0, -2))


def ring_owner(n, k):
    me = lax.axis_index("feat")
    place = jnp.where(lax.rem(me, 2) == 0, lax.div(me, 2), n - 1 - lax.div(me, 2))
    place = lax.rem(place + k, n)
    return jnp.where(place < n // 2, 2 * place, 2 * (n - 1 - place) + 1)


def row_starts(n, rows, width):
    core = lax.axis_index("corp")
    half = width // 2
    return [
        ring_owner(n, jnp.where(core == 0, k, n - k)) * width + (1 - core if flip else core) * half for k, flip in rows
    ]


def stream(n, rows, blocks, loads, m_ref, tiles, sems, acc_refs, behind=()):
    slots, depth, width = tiles.shape
    counts = [b[0].shape[1] // depth for b in blocks]
    total = sum(counts)
    starts = row_starts(n, rows, width)

    def copy(i, start):
        slot = lax.rem(i, slots)
        at = pl.ds(pl.multiple_of(start, depth), depth)
        return pltpu.make_async_copy(m_ref.at[at, :], tiles.at[slot], sems.at[slot])

    def start_of(i):
        row, base = starts[0] + i * depth, counts[0]
        for b in range(1, len(blocks)):
            row = jnp.where(i >= base, starts[b] + (i - base) * depth, row)
            base += counts[b]
        return row

    for i in range(min(slots, total)):
        copy(i, start_of(i)).start()
    for other in behind:
        other.start()
    first = 0
    for block, count in zip(blocks, counts):
        for load in loads[: len(block)]:
            load.wait()
        loads = loads[len(block) :]

        def step(j, carry, block=block, first=first):
            i = first + j
            copy(i, 0).wait()
            at = pl.ds(pl.multiple_of(j * depth, depth), depth)
            piece = jnp.concatenate([ref[:, at] for ref in block], 0)
            product = dot(piece, tiles[lax.rem(i, slots)])
            docs = block[0].shape[0]
            for k, acc_ref in enumerate(acc_refs):
                acc_ref[...] += product[k * docs : (k + 1) * docs]

            @pl.when(i + slots < total)
            def _():
                copy(i + slots, start_of(i + slots)).start()

            return carry

        lax.fori_loop(0, count, step, 0)
        first += count


def load_pieces(sources, pieces, sems):
    loads = [pltpu.make_async_copy(ref, pieces.at[i], sems.at[i]) for i, ref in enumerate(sources)]
    for load in loads:
        load.start()
    return loads


def apply_kernel(n, rows, sets, n_kept, keep, *refs):
    count = sets * len(rows)
    m_ref, outs, (pieces, piece_sems, tiles, sems, keep_sems) = refs[count], refs[-5 - sets - n_kept : -5], refs[-5:]
    out_refs, kept = outs[:sets], outs[sets:]
    loads = load_pieces(refs[:count], pieces, piece_sems)
    copies = []
    if keep:
        for out_ref in out_refs:
            out_ref[...] = jnp.zeros_like(out_ref)
        height = kept[0].shape[0]
        starts = row_starts(n, keep, m_ref.shape[1])
        for i in range(n_kept):
            first, part = divmod(i * len(keep), n_kept)
            row = starts[first] + part // len(keep) * height
            at = pl.ds(pl.multiple_of(row, height), height)
            copies.append(pltpu.make_async_copy(m_ref.at[at, :], kept[i], keep_sems.at[i]))
    blocks = [[pieces.at[b * sets + k] for k in range(sets)] for b in range(len(rows))]
    stream(n, rows, blocks, loads, m_ref, tiles, sems, out_refs, copies)
    for copy in copies:
        copy.wait()


def score_kernel(n_pieces, n_kept, n_parts, *refs):
    in_ref, other_ref, *kept = refs[n_pieces : n_pieces + 2 + n_kept]
    q_refs, (out_ref, acc, pair, queries, q_sems, pieces, piece_sems) = refs[n_pieces + 2 + n_kept : -7], refs[-7:]
    loads = load_pieces(refs[:n_pieces], pieces, piece_sems)
    q_loads = load_pieces(q_refs, queries, q_sems)
    acc[...] = in_ref[...] + other_ref[...]
    each, depth = n_kept // n_pieces, kept[0].shape[0]
    for i in range(n_pieces):
        loads[i].wait()
        for j in range(each):
            acc[...] += dot(pieces[i, :, j * depth : (j + 1) * depth], kept[i * each + j][...])
    docs = acc.shape[0]
    hi = acc[...].astype(BF16)
    pair[:docs, :] = hi
    pair[docs:, :] = (acc[...] - hi.astype(F32)).astype(BF16)
    height = queries.shape[1]
    for k in range(n_parts):
        q_loads[k].wait()
        place = lax.rem(lax.axis_index("corp") + n_parts - k, n_parts)
        both = dot_t(queries[k], pair[...])
        out_ref[pl.ds(pl.multiple_of(place * height, height), height), :] = both[:, :docs] + both[:, docs:]


VMEM = pl.BlockSpec(memory_space=pltpu.VMEM)
ANY = pl.BlockSpec(memory_space=pl.ANY)


def call(kernel, out_shape, operands, specs, scratch, flops, n_bytes, aliases):
    return pl.pallas_call(
        kernel,
        out_shape=out_shape,
        in_specs=specs,
        out_specs=jax.tree.map(lambda _: VMEM, out_shape),
        scratch_shapes=scratch,
        input_output_aliases=aliases,
        cost_estimate=pl.CostEstimate(flops=flops, bytes_accessed=n_bytes, transcendentals=0),
        compiler_params=pltpu.CompilerParams(vmem_limit_bytes=24 << 20),
    )(*operands)


def piece_scratch(pieces):
    return [pltpu.VMEM((len(pieces),) + pieces[0].shape, BF16), pltpu.SemaphoreType.DMA((len(pieces),))]


def apply(n, accs, kept, blocks, rows, m, keep=()):
    pieces = [p for b in blocks for p in b]
    sets = len(blocks[0])
    docs, span = pieces[0].shape
    depth = min(TILE_ROWS, span)
    n_kept = len(keep) * span // KEPT_ROWS if keep else len(kept)
    shape = [jax.ShapeDtypeStruct((docs, m.shape[1]), F32)] * sets
    shape += [jax.ShapeDtypeStruct((KEPT_ROWS, m.shape[1]), BF16)] * n_kept
    carried = [] if keep else accs + kept
    scratch = piece_scratch(pieces) + [
        pltpu.VMEM((SLOTS, depth, m.shape[1]), BF16),
        pltpu.SemaphoreType.DMA((SLOTS,)),
        pltpu.SemaphoreType.DMA((n_kept,)),
    ]
    outs = call(
        functools.partial(apply_kernel, n, rows, sets, n_kept, keep),
        shape,
        pieces + [m] + carried,
        [ANY] * (len(pieces) + 1) + [VMEM] * len(carried),
        scratch,
        2 * docs * len(pieces) * span * m.shape[1],
        2 * (len(rows) + len(keep)) * span * m.shape[1],
        {len(pieces) + 1 + k: k for k in range(len(carried))},
    )
    return list(outs[:sets]), list(outs[sets:])


def score(accs, kept, pieces, parts):
    queries = sum(p.shape[0] for p in parts)
    docs, width = accs[0].shape
    scratch = [
        pltpu.VMEM((docs, width), F32),
        pltpu.VMEM((2 * docs, width), BF16),
        *piece_scratch(parts),
        *piece_scratch(pieces),
    ]
    return call(
        functools.partial(score_kernel, len(pieces), len(kept), len(parts)),
        jax.ShapeDtypeStruct((queries, docs), F32),
        pieces + accs + kept + parts,
        [ANY] * len(pieces) + [VMEM] * (2 + len(kept)) + [ANY] * len(parts),
        scratch,
        2 * docs * width * (2 * queries + len(pieces) * pieces[0].shape[1]),
        2 * queries * width,
        {},
    )


def scatter_sum(s, n, me):
    x, z, m = lax.rem(me, 2), lax.div(me, 2), n // 2
    s = s.reshape((m, 2) + s.shape[1:])
    mine = lax.dynamic_index_in_dim(s, x, 1, False)
    theirs = lax.dynamic_index_in_dim(s, 1 - x, 1, False)
    s = mine + lax.ppermute(theirs, "feat", [(i, i ^ 1) for i in range(n)])
    out = lax.dynamic_index_in_dim(s, z, 0, False)
    for k in range(1, m):
        y = lax.dynamic_index_in_dim(s, lax.rem(z + k, m), 0, False)
        out = out + lax.ppermute(y, "feat", [(i, (i + 2 * k) % n) for i in range(n)])
    return out


def ring_body(n, q, m, d):
    docs, width = d.shape
    half = width // 2
    far = n // 2
    order = ring_order(n)
    d, me, core = lax.optimization_barrier((d, lax.axis_index("feat"), lax.axis_index("corp")))

    def move(x, shift, cross):
        pairs = [
            (2 * order[p] + c, 2 * order[(p + shift(c)) % n] + (c ^ cross)) for p in range(n) for c in range(2)
        ]
        return lax.ppermute(x, ("feat", "corp"), pairs)

    def fore(c):
        return 1 - 2 * c

    def back(c):
        return 2 * c - 1

    p_fore = p_back = lax.dynamic_slice(d, (0, core * half), (docs, half))
    r_fore = r_back = lax.dynamic_slice(d, (0, (1 - core) * half), (docs, half))
    own_p = p_fore
    own_r = move(r_fore, lambda c: 0, 1)
    parts = [q, lax.ppermute(q, "corp", [(0, 1), (1, 0)])]
    accs, kept = [], []
    blocks, rows = [(own_p, own_r)], [(0, False)]
    last_rows = [(far, False), (far, True)]
    for s in range(1, far):
        r_ways = (back, fore) if s == 1 else (fore, back)
        r_fore = move(r_fore, r_ways[0], s == 1)
        r_back = move(r_back, r_ways[1], s == 1)
        p_fore, p_back = move(p_fore, fore, 0), move(p_back, back, 0)
        accs, kept = apply(n, accs, kept, blocks, rows, m, last_rows if s == 1 else ())
        blocks, rows = [(p_fore, r_fore), (p_back, r_back)], [(n - s, False), (s, False)]

    mine, theirs = accs
    z_r, z_p = move(r_fore, fore, 1), move(p_fore, fore, 0)
    (theirs,), kept = apply(n, [theirs], kept, [(r_fore,), (r_back,)], rows, m)
    other = lax.ppermute(theirs, "corp", [(0, 1), (1, 0)])
    (mine,), kept = apply(n, [mine], kept, [(p_fore,), (p_back,)], rows, m)
    scores = score([mine, other], kept, [z_p, z_r], parts)
    scores, me = lax.optimization_barrier((scores, me))
    return scatter_sum(scores.reshape(n, -1, docs), n, me)


def plain_body(q, m, d):
    applied = dot(lax.all_gather(d, "feat", axis=1, tiled=True), m)
    left = lax.all_gather(q, "corp", axis=0, tiled=True).astype(F32)
    scores = lax.dot_general(
        left, applied, (((1,), (1,)), ((), ())), precision=lax.Precision.HIGHEST, preferred_element_type=F32
    )
    return lax.psum_scatter(scores, "feat", scatter_dimension=0, tiled=True)


def solution(mesh):
    n, n_corp = mesh.shape["feat"], mesh.shape["corp"]
    ring = n % 4 == 0 and 8 <= n <= 16 and n_corp == 2

    def on_device(q, m, d):
        if not ring:
            return plain_body(q, m, d)
        return ring_body(n, q, m, d)

    placed = (P(("groups", "corp"), "feat"), P(None, "feat"), P(("groups", "corp"), "feat"))
    return jax.shard_map(
        on_device,
        mesh=mesh,
        in_specs=placed,
        out_specs=P(("groups", "feat"), "corp"),
        check_vma=False,
    )
```

time: 78.1 us -> 78 us (level)
  starting transfers between devices: 31.9 us -> 26.7 us
  waiting for transfers between devices: 20.2 us -> 23.2 us
  Pallas kernels: 23.8 us -> 26.1 us
    ppermute x15, starting transfers between devices: 23.3 us -> 18.6 us  [move(): return lax.ppermute(x, ('feat', 'corp'), pairs)]
    ppermute x15, waiting for transfers between devices: 11.2 us -> 14.3 us  [move(): return lax.ppermute(x, ('feat', 'corp'), pairs)]
    pallas_call x6, Pallas kernels: 23.8 us -> 26.1 us  [call(): pl.pallas_call(kernel, out_shape=out_shape, in_specs=specs, out_specs=jax...]
    ppermute x1, starting transfers between devices: 1.8 us -> 0.07 us  [ring_body(): other = lax.ppermute(theirs, 'corp', [(0, 1), (1, 0)])]
    ppermute x1, starting transfers between devices: 0.07 us -> 1.08 us  [scatter_sum(): s = mine + lax.ppermute(theirs, 'feat', [(i, i ^ 1) for i in range(n)])]
  transfers between devices with their start and end apart: 21 -> 21, of which waited for: 7 -> 9; matrix products, arithmetic and copies ran while one was open for 0% -> 0% of each run, Pallas kernels for 27% -> 29%
where the time goes in v3:
time: 78 us; the launch traced here: 77.9 us
  starting transfers between devices  26.7 us (34%)
  Pallas kernels  26.1 us (33%)
  waiting for transfers between devices  23.2 us (30%)
  local copies, waits for them, and re-layouts  1.11 us (1%)
    pallas_call x6, Pallas kernels, call(): pl.pallas_call(kernel, out_shape=out_shape, in_specs=specs, out_specs=jax...  26.1 us
    ppermute x15, starting transfers between devices, move(): return lax.ppermute(x, ('feat', 'corp'), pairs)  18.6 us
    ppermute x15, waiting for transfers between devices, move(): return lax.ppermute(x, ('feat', 'corp'), pairs)  14.3 us
    ppermute x3, starting transfers between devices, scatter_sum(): lax.ppermute(y, 'feat', [(i, (i + 2 * k) % n) for i in range(n)])  6.15 us
    ppermute x1, waiting for transfers between devices, scatter_sum(): s = mine + lax.ppermute(theirs, 'feat', [(i, i ^ 1) for i in range(n)])  6.09 us
    ppermute x3, waiting for transfers between devices, scatter_sum(): lax.ppermute(y, 'feat', [(i, (i + 2 * k) % n) for i in range(n)])  2.77 us
  transfers between devices with their start and end apart: 21, of which 9 were waited for; matrix products, arithmetic and copies ran while one was open for 0% of the time, Pallas kernels for 29%

profile of v3, /device:TPU:0, one launch (start us, length us, event | category | flops | bytes accessed | tf_op | source)
XLA Modules:
  0.0 77.9 jit_solution(10571649889688716582)
XLA Ops:
  0.0 1.1 %constant_dynamic-slice_fusion = (bf16[128,1024]{1,0:T(8,128)(2,1)S(1)}, bf16[128,1024]{1,0:T(8,128)(2,1)S(1)}) fusion(bf16[128,2048]{1,0:T(8,128)(2,1)} %param.5, s32[]{:T(128)S(6)} %select_n.27, s32[]{:T(128)S(6)} %select_n.26), kind=kLoop, calls=%fused_computation.8 | loop fusion | bytes 1048584 | tf_op jit(solution)/shard_map/dynamic_slice | solution.py:247
  1.1 2.5 %collective-permute-start.4 = (bf16[128,1024]{1,0:T(8,128)(2,1)S(1)}, bf16[128,1024]{1,0:T(8,128)(2,1)S(1)}, u32[]{:S(2)}, u32[]{:S(2)}) collective-permute-start(bf16[128,1024]{1,0:T(8,128)(2,1)S(1)} %get-tuple-element.51), channel_id=1, source_target_pairs={{0,3},{1,4},{4,1},{5,8},{8,5},{9,12},{12,9},{13,14},{14,13},{15,10... | collective-permute-start | bytes 786440 | tf_op jit(solution)/shard_map/ppermute | solution.py:238
  3.5 1.9 %collective-permute-start.11 = (bf16[128,1024]{1,0:T(8,128)(2,1)S(1)}, bf16[128,1024]{1,0:T(8,128)(2,1)S(1)}, u32[]{:S(2)}, u32[]{:S(2)}) collective-permute-start(bf16[128,1024]{1,0:T(8,128)(2,1)S(1)} %get-tuple-element.51), channel_id=1, source_target_pairs={{0,5},{1,2},{4,9},{5,0},{8,13},{9,4},{12,15},{13,8},{14,11},{15,12... | collective-permute-start | bytes 786440 | tf_op jit(solution)/shard_map/ppermute | solution.py:238
  5.5 1.6 %collective-permute-start = (bf16[128,1024]{1,0:T(8,128)(2,1)S(1)}, bf16[128,1024]{1,0:T(8,128)(2,1)S(1)}, u32[]{:S(2)}, u32[]{:S(2)}) collective-permute-start(bf16[128,1024]{1,0:T(8,128)(2,1)S(1)} %get-tuple-element.52.refs_0_), channel_id=1, source_target_pairs={{0,4},{1,3},{4,8},{5,1},{8,12},{9,5},{12,14},{13,9},{14,10},{15,13... | collective-permute-start | bytes 786440 | tf_op jit(solution)/shard_map/ppermute | solution.py:238
  7.1 0.4 collective-permute-start.8
  7.5 1.7 %collective-permute-done.4.refs_1_ = bf16[128,1024]{1,0:T(8,128)(2,1)S(1)} collective-permute-done((bf16[128,1024]{1,0:T(8,128)(2,1)S(1)}, bf16[128,1024]{1,0:T(8,128)(2,1)S(1)}, u32[]{:S(2)}, u32[]{:S(2)}) %collective-permute-start.4) | collective-permute-done | bytes 262176 | tf_op jit(solution)/shard_map/ppermute | solution.py:238
  9.2 1.7 %collective-permute-start.5 = (bf16[128,1024]{1,0:T(8,128)(2,1)S(1)}, bf16[128,1024]{1,0:T(8,128)(2,1)S(1)}, u32[]{:S(2)}, u32[]{:S(2)}) collective-permute-start(bf16[128,1024]{1,0:T(8,128)(2,1)S(1)} %collective-permute-done.4.refs_1_), channel_id=1, source_target_pairs={{0,4},{1,3},{4,8},{5,1},{8,12},{9,5},{12,14},{13,9},{14,10},{15,13... | collective-permute-start | bytes 786440 | tf_op jit(solution)/shard_map/ppermute | solution.py:238
  10.9 1.3 %collective-permute-done.11.refs_3_ = bf16[128,1024]{1,0:T(8,128)(2,1)S(1)} collective-permute-done((bf16[128,1024]{1,0:T(8,128)(2,1)S(1)}, bf16[128,1024]{1,0:T(8,128)(2,1)S(1)}, u32[]{:S(2)}, u32[]{:S(2)}) %collective-permute-start.11) | collective-permute-done | bytes 262176 | tf_op jit(solution)/shard_map/ppermute | solution.py:238
  12.2 1.5 %collective-permute-start.12 = (bf16[128,1024]{1,0:T(8,128)(2,1)S(1)}, bf16[128,1024]{1,0:T(8,128)(2,1)S(1)}, u32[]{:S(2)}, u32[]{:S(2)}) collective-permute-start(bf16[128,1024]{1,0:T(8,128)(2,1)S(1)} %collective-permute-done.11.refs_3_), channel_id=1, source_target_pairs={{0,2},{1,5},{4,0},{5,9},{8,4},{9,13},{12,8},{13,15},{14,12},{15,11... | collective-permute-start | bytes 786440 | tf_op jit(solution)/shard_map/ppermute | solution.py:238
  13.7 0.8 %collective-permute-start.16 = (bf16[384,2048]{1,0:T(8,128)(2,1)}, bf16[384,2048]{1,0:T(8,128)(2,1)S(1)}, u32[]{:S(2)}, u32[]{:S(2)}) collective-permute-start(bf16[384,2048]{1,0:T(8,128)(2,1)} %refs_6_.1), channel_id=1, source_target_pairs={{0,1},{1,0},{2,3},{3,2},{4,5},{5,4},{6,7},{7,6},{8,9},{9,8},{10,11... | collective-permute-start | bytes 4718600 | tf_op jit(solution)/shard_map/ppermute | solution.py:250
  14.5 2.7 %collective-permute-done.refs_0_ = bf16[128,1024]{1,0:T(8,128)(2,1)S(1)} collective-permute-done((bf16[128,1024]{1,0:T(8,128)(2,1)S(1)}, bf16[128,1024]{1,0:T(8,128)(2,1)S(1)}, u32[]{:S(2)}, u32[]{:S(2)}) %collective-permute-start) | collective-permute-done | bytes 262176 | tf_op jit(solution)/shard_map/ppermute | solution.py:238
  17.2 2.2 %collective-permute-start.1 = (bf16[128,1024]{1,0:T(8,128)(2,1)S(1)}, bf16[128,1024]{1,0:T(8,128)(2,1)S(1)}, u32[]{:S(2)}, u32[]{:S(2)}) collective-permute-start(bf16[128,1024]{1,0:T(8,128)(2,1)S(1)} %collective-permute-done.refs_0_), channel_id=1, source_target_pairs={{0,4},{1,3},{4,8},{5,1},{8,12},{9,5},{12,14},{13,9},{14,10},{15,13... | collective-permute-start | bytes 786440 | tf_op jit(solution)/shard_map/ppermute | solution.py:238
  19.5 4.8 %shard_map.37 = (f32[128,2048]{1,0:T(8,128)S(1)}, f32[128,2048]{1,0:T(8,128)S(1)}, bf16[1024,2048]{1,0:T(8,128)(2,1)S(1)}, bf16[1024,2048]{1,0:T(8,128)(2,1)S(1)}) custom-call(bf16[128,1024]{1,0:T(8,128)(2,1)S(1)} %get-tuple-element.52.refs_0_, bf16[128,1024]{1,0:T(8,128)(2,1)S(1)} %collective-permute-done.13.refs_1_, bf16[16384,2048]{1,0:T(8,128)(2,1)} %refs_2_.5), custom_call_target="tpu_custom_call" | custom-call | flops 1073741824 | bytes 12582912 | tf_op jit(solution)/shard_map/pallas_call | solution.py:150
  24.3 2.1 %collective-permute-start.6 = (bf16[128,1024]{1,0:T(8,128)(2,1)S(1)}, bf16[128,1024]{1,0:T(8,128)(2,1)S(1)}, u32[]{:S(2)}, u32[]{:S(2)}) collective-permute-start(bf16[128,1024]{1,0:T(8,128)(2,1)S(1)} %collective-permute-done.5.refs_1_), channel_id=1, source_target_pairs={{0,4},{1,3},{4,8},{5,1},{8,12},{9,5},{12,14},{13,9},{14,10},{15,13... | collective-permute-start | bytes 786440 | tf_op jit(solution)/shard_map/ppermute | solution.py:238
  26.4 4.7 %shard_map.38 = (f32[128,2048]{1,0:T(8,128)S(1)}, f32[128,2048]{1,0:T(8,128)S(1)}, bf16[1024,2048]{1,0:T(8,128)(2,1)S(1)}, bf16[1024,2048]{1,0:T(8,128)(2,1)S(1)}) custom-call(bf16[128,1024]{1,0:T(8,128)(2,1)S(1)} %collective-permute-done.refs_0_, ...), custom_call_target="tpu_custom_call", output_to_operand_aliasing={{0}: (5, {}), {1}: (6, {}), {2}: (7, {}), {3}: (8, {})} | custom-call | flops 2147483648 | bytes 8388608 | tf_op jit(solution)/shard_map/pallas_call | solution.py:150
  31.1 4.7 %shard_map.39 = (f32[128,2048]{1,0:T(8,128)S(1)}, f32[128,2048]{1,0:T(8,128)S(1)}, bf16[1024,2048]{1,0:T(8,128)(2,1)S(1)}, bf16[1024,2048]{1,0:T(8,128)(2,1)S(1)}) custom-call(bf16[128,1024]{1,0:T(8,128)(2,1)S(1)} %collective-permute-done.1.refs_0_, ...), custom_call_target="tpu_custom_call", output_to_operand_aliasing={{0}: (5, {}), {1}: (6, {}), {2}: (7, {}), {3}: (8, {})} | custom-call | flops 2147483648 | bytes 8388608 | tf_op jit(solution)/shard_map/pallas_call | solution.py:150
  35.8 4.1 %shard_map.40 = (f32[128,2048]{1,0:T(8,128)S(1)}, bf16[1024,2048]{1,0:T(8,128)(2,1)S(1)}, bf16[1024,2048]{1,0:T(8,128)(2,1)S(1)}) custom-call(bf16[128,1024]{1,0:T(8,128)(2,1)S(1)} %collective-permute-done.6.refs_0_, bf16[128,1024]{1,0:T(8,128)(2,1)S(1)} %collective-permute-done.14.refs_1_, ...), custom_call_target="tpu_custom_call", output_to_operand_aliasing={{0}: (3, {}), {1}: (4, {}), {2}: (5, {})} | custom-call | flops 1073741824 | bytes 8388608 | tf_op jit(solution)/shard_map/pallas_call | solution.py:150
  40.0 2.0 %collective-permute-start.2 = (bf16[128,1024]{1,0:T(8,128)(2,1)S(1)}, bf16[128,1024]{1,0:T(8,128)(2,1)S(1)}, u32[]{:S(2)}, u32[]{:S(2)}) collective-permute-start(bf16[128,1024]{1,0:T(8,128)(2,1)S(1)} %collective-permute-done.1.refs_0_), channel_id=1, source_target_pairs={{0,4},{1,3},{4,8},{5,1},{8,12},{9,5},{12,14},{13,9},{14,10},{15,13... | collective-permute-start | bytes 786440 | tf_op jit(solution)/shard_map/ppermute | solution.py:238
  42.0 6.1 %collective-permute-done.2.refs_0_ = bf16[128,1024]{1,0:T(8,128)(2,1)S(1)} collective-permute-done((bf16[128,1024]{1,0:T(8,128)(2,1)S(1)}, bf16[128,1024]{1,0:T(8,128)(2,1)S(1)}, u32[]{:S(2)}, u32[]{:S(2)}) %collective-permute-start.2) | collective-permute-done | bytes 262176 | tf_op jit(solution)/shard_map/ppermute | solution.py:238
  48.1 2.5 %collective-permute-start.3 = (bf16[128,1024]{1,0:T(8,128)(2,1)S(1)}, bf16[128,1024]{1,0:T(8,128)(2,1)S(1)}, u32[]{:S(2)}, u32[]{:S(2)}) collective-permute-start(bf16[128,1024]{1,0:T(8,128)(2,1)S(1)} %collective-permute-done.2.refs_0_), channel_id=1, source_target_pairs={{0,4},{1,3},{4,8},{5,1},{8,12},{9,5},{12,14},{13,9},{14,10},{15,13... | collective-permute-start | bytes 786440 | tf_op jit(solution)/shard_map/ppermute | solution.py:238
  50.6 4.2 %shard_map.41 = (f32[128,2048]{1,0:T(8,128)S(1)}, bf16[1024,2048]{1,0:T(8,128)(2,1)S(1)}, bf16[1024,2048]{1,0:T(8,128)(2,1)S(1)}) custom-call(bf16[128,1024]{1,0:T(8,128)(2,1)S(1)} %collective-permute-done.2.refs_0_, bf16[128,1024]{1,0:T(8,128)(2,1)S(1)} %collective-permute-done.10.refs_1_, ...), custom_call_target="tpu_custom_call", output_to_operand_aliasing={{0}: (3, {}), {1}: (4, {}), {2}: (5, {})} | custom-call | flops 1073741824 | bytes 8388608 | tf_op jit(solution)/shard_map/pallas_call | solution.py:150
  54.8 2.5 %collective-permute-done.7.refs_1_ = bf16[128,1024]{1,0:T(8,128)(2,1)S(1)} collective-permute-done((bf16[128,1024]{1,0:T(8,128)(2,1)S(1)}, bf16[128,1024]{1,0:T(8,128)(2,1)S(1)}, u32[]{:S(2)}, u32[]{:S(2)}) %collective-permute-start.7) | collective-permute-done | bytes 262176 | tf_op jit(solution)/shard_map/ppermute | solution.py:238
  57.3 3.7 %shard_map.42 = f32[768,128]{1,0:T(8,128)S(1)} custom-call(bf16[128,1024]{1,0:T(8,128)(2,1)S(1)} %collective-permute-done.3.refs_0_, bf16[128,1024]{1,0:T(8,128)(2,1)S(1)} %collective-permute-done.7.refs_1_, f32[128,2048]{1,0:T(8,128)S(1)} %get-tuple-element.44.refs_2_, f32[128,2048]{1,0:T(8,128)S(1)} %collective-permute-done.15.refs_3_, ...), custom_call_target="tpu_custom_call" | custom-call | flops 1879048192 | bytes 3145728 | tf_op jit(solution)/shard_map/pallas_call | solution.py:150
  61.1 1.1 %collective-permute-start.17 = (f32[4,96,128]{2,1,0:T(8,128)S(1)}, f32[4,96,128]{2,1,0:T(8,128)S(1)}, u32[]{:S(2)}, u32[]{:S(2)}) collective-permute-start(f32[4,96,128]{2,1,0:T(8,128)S(1)} %dynamic-slice_bitcast_fusion), channel_id=1, source_target_pairs={{0,2},{2,0},{4,6},{6,4},{8,10},{10,8},{12,14},{14,12},{1,3},{3,1},... | collective-permute-start | bytes 589832 | tf_op jit(solution)/shard_map/ppermute | solution.py:219
  62.2 6.1 %collective-permute-done.17 = f32[4,96,128]{2,1,0:T(8,128)S(1)} collective-permute-done((f32[4,96,128]{2,1,0:T(8,128)S(1)}, f32[4,96,128]{2,1,0:T(8,128)S(1)}, u32[]{:S(2)}, u32[]{:S(2)}) %collective-permute-start.17) | collective-permute-done | bytes 196640 | tf_op jit(solution)/shard_map/ppermute | solution.py:219
  68.3 2.1 %collective-permute-start.18 = (f32[96,128]{1,0:T(8,128)S(1)}, f32[96,128]{1,0:T(8,128)S(1)}, u32[]{:S(2)}, u32[]{:S(2)}) collective-permute-start(f32[96,128]{1,0:T(8,128)S(1)} %get-tuple-element.53), channel_id=1, source_target_pairs={{0,4},{2,6},{4,8},{6,10},{8,12},{10,14},{12,0},{14,2},{1,5},{3,7},... | collective-permute-start | bytes 147464 | tf_op jit(solution)/shard_map/ppermute | solution.py:223
  70.4 2.7 %collective-permute-start.19 = (f32[96,128]{1,0:T(8,128)S(1)}, f32[96,128]{1,0:T(8,128)S(1)}, u32[]{:S(2)}, u32[]{:S(2)}) collective-permute-start(f32[96,128]{1,0:T(8,128)S(1)} %get-tuple-element.55), channel_id=1, source_target_pairs={{0,8},{2,10},{4,12},{6,14},{8,0},{10,2},{12,4},{14,6},{1,9},{3,11}... | collective-permute-start | bytes 147464 | tf_op jit(solution)/shard_map/ppermute | solution.py:223
  73.2 1.3 %collective-permute-start.20 = (f32[96,128]{1,0:T(8,128)S(1)}, f32[96,128]{1,0:T(8,128)S(1)}, u32[]{:S(2)}, u32[]{:S(2)}) collective-permute-start(f32[96,128]{1,0:T(8,128)S(1)} %get-tuple-element.54), channel_id=1, source_target_pairs={{0,12},{2,14},{4,0},{6,2},{8,4},{10,6},{12,8},{14,10},{1,13},{3,15... | collective-permute-start | bytes 147464 | tf_op jit(solution)/shard_map/ppermute | solution.py:223
  74.5 0.2 collective-permute-done.18
  74.7 2.1 %collective-permute-done.19 = f32[96,128]{1,0:T(8,128)S(1)} collective-permute-done((f32[96,128]{1,0:T(8,128)S(1)}, f32[96,128]{1,0:T(8,128)S(1)}, u32[]{:S(2)}, u32[]{:S(2)}) %collective-permute-start.19) | collective-permute-done | bytes 49184 | tf_op jit(solution)/shard_map/ppermute | solution.py:223
  76.8 0.5 collective-permute-done.20
  77.3 0.6 fusion.1
  (23 shorter events, 0.4 us)
Async XLA Ops:
  1.1 8.2 %collective-permute-start.4 = (bf16[128,1024]{1,0:T(8,128)(2,1)S(1)}, bf16[128,1024]{1,0:T(8,128)(2,1)S(1)}, u32[]{:S(2)}, u32[]{:S(2)}) collective-permute-start(bf16[128,1024]{1,0:T(8,128)(2,1)S(1)} %get-tuple-element.51), channel_id=1, source_target_pairs={{0,3},{1,4},{4,1},{5,8},{8,5},{9,12},{12,9},{13,14},{14,13},{15,10... | collective-permute-start | bytes 786440 | tf_op jit(solution)/shard_map/ppermute | solution.py:238
  3.5 8.6 %collective-permute-start.11 = (bf16[128,1024]{1,0:T(8,128)(2,1)S(1)}, bf16[128,1024]{1,0:T(8,128)(2,1)S(1)}, u32[]{:S(2)}, u32[]{:S(2)}) collective-permute-start(bf16[128,1024]{1,0:T(8,128)(2,1)S(1)} %get-tuple-element.51), channel_id=1, source_target_pairs={{0,5},{1,2},{4,9},{5,0},{8,13},{9,4},{12,15},{13,8},{14,11},{15,12... | collective-permute-start | bytes 786440 | tf_op jit(solution)/shard_map/ppermute | solution.py:238
  5.5 8.2 %collective-permute-start.13 = (bf16[128,1024]{1,0:T(8,128)(2,1)S(1)}, bf16[128,1024]{1,0:T(8,128)(2,1)S(1)}, u32[]{:S(2)}, u32[]{:S(2)}) collective-permute-start(bf16[128,1024]{1,0:T(8,128)(2,1)S(1)} %get-tuple-element.51), channel_id=1, source_target_pairs={{0,1},{1,0},{4,5},{5,4},{8,9},{9,8},{12,13},{13,12},{14,15},{15,14... | collective-permute-start | bytes 786440 | tf_op jit(solution)/shard_map/ppermute | solution.py:238
  5.5 11.7 %collective-permute-start = (bf16[128,1024]{1,0:T(8,128)(2,1)S(1)}, bf16[128,1024]{1,0:T(8,128)(2,1)S(1)}, u32[]{:S(2)}, u32[]{:S(2)}) collective-permute-start(bf16[128,1024]{1,0:T(8,128)(2,1)S(1)} %get-tuple-element.52.refs_0_), channel_id=1, source_target_pairs={{0,4},{1,3},{4,8},{5,1},{8,12},{9,5},{12,14},{13,9},{14,10},{15,13... | collective-permute-start | bytes 786440 | tf_op jit(solution)/shard_map/ppermute | solution.py:238
  7.1 12.4 %collective-permute-start.8 = (bf16[128,1024]{1,0:T(8,128)(2,1)S(1)}, bf16[128,1024]{1,0:T(8,128)(2,1)S(1)}, u32[]{:S(2)}, u32[]{:S(2)}) collective-permute-start(bf16[128,1024]{1,0:T(8,128)(2,1)S(1)} %get-tuple-element.52.refs_0_), channel_id=1, source_target_pairs={{0,2},{1,5},{4,0},{5,9},{8,4},{9,13},{12,8},{13,15},{14,12},{15,11... | collective-permute-start | bytes 786440 | tf_op jit(solution)/shard_map/ppermute | solution.py:238
  9.2 15.0 %collective-permute-start.5 = (bf16[128,1024]{1,0:T(8,128)(2,1)S(1)}, bf16[128,1024]{1,0:T(8,128)(2,1)S(1)}, u32[]{:S(2)}, u32[]{:S(2)}) collective-permute-start(bf16[128,1024]{1,0:T(8,128)(2,1)S(1)} %collective-permute-done.4.refs_1_), channel_id=1, source_target_pairs={{0,4},{1,3},{4,8},{5,1},{8,12},{9,5},{12,14},{13,9},{14,10},{15,13... | collective-permute-start | bytes 786440 | tf_op jit(solution)/shard_map/ppermute | solution.py:238
  12.2 14.1 %collective-permute-start.12 = (bf16[128,1024]{1,0:T(8,128)(2,1)S(1)}, bf16[128,1024]{1,0:T(8,128)(2,1)S(1)}, u32[]{:S(2)}, u32[]{:S(2)}) collective-permute-start(bf16[128,1024]{1,0:T(8,128)(2,1)S(1)} %collective-permute-done.11.refs_3_), channel_id=1, source_target_pairs={{0,2},{1,5},{4,0},{5,9},{8,4},{9,13},{12,8},{13,15},{14,12},{15,11... | collective-permute-start | bytes 786440 | tf_op jit(solution)/shard_map/ppermute | solution.py:238
  13.7 43.6 %collective-permute-start.16 = (bf16[384,2048]{1,0:T(8,128)(2,1)}, bf16[384,2048]{1,0:T(8,128)(2,1)S(1)}, u32[]{:S(2)}, u32[]{:S(2)}) collective-permute-start(bf16[384,2048]{1,0:T(8,128)(2,1)} %refs_6_.1), channel_id=1, source_target_pairs={{0,1},{1,0},{2,3},{3,2},{4,5},{5,4},{6,7},{7,6},{8,9},{9,8},{10,11... | collective-permute-start | bytes 4718600 | tf_op jit(solution)/shard_map/ppermute | solution.py:250
  17.2 13.8 %collective-permute-start.1 = (bf16[128,1024]{1,0:T(8,128)(2,1)S(1)}, bf16[128,1024]{1,0:T(8,128)(2,1)S(1)}, u32[]{:S(2)}, u32[]{:S(2)}) collective-permute-start(bf16[128,1024]{1,0:T(8,128)(2,1)S(1)} %collective-permute-done.refs_0_), channel_id=1, source_target_pairs={{0,4},{1,3},{4,8},{5,1},{8,12},{9,5},{12,14},{13,9},{14,10},{15,13... | collective-permute-start | bytes 786440 | tf_op jit(solution)/shard_map/ppermute | solution.py:238
  19.4 11.6 %collective-permute-start.9 = (bf16[128,1024]{1,0:T(8,128)(2,1)S(1)}, bf16[128,1024]{1,0:T(8,128)(2,1)S(1)}, u32[]{:S(2)}, u32[]{:S(2)}) collective-permute-start(bf16[128,1024]{1,0:T(8,128)(2,1)S(1)} %collective-permute-done.8.refs_2_), channel_id=1, source_target_pairs={{0,2},{1,5},{4,0},{5,9},{8,4},{9,13},{12,8},{13,15},{14,12},{15,11... | collective-permute-start | bytes 786440 | tf_op jit(solution)/shard_map/ppermute | solution.py:238
  24.3 11.5 %collective-permute-start.6 = (bf16[128,1024]{1,0:T(8,128)(2,1)S(1)}, bf16[128,1024]{1,0:T(8,128)(2,1)S(1)}, u32[]{:S(2)}, u32[]{:S(2)}) collective-permute-start(bf16[128,1024]{1,0:T(8,128)(2,1)S(1)} %collective-permute-done.5.refs_1_), channel_id=1, source_target_pairs={{0,4},{1,3},{4,8},{5,1},{8,12},{9,5},{12,14},{13,9},{14,10},{15,13... | collective-permute-start | bytes 786440 | tf_op jit(solution)/shard_map/ppermute | solution.py:238
  26.3 9.5 %collective-permute-start.14 = (bf16[128,1024]{1,0:T(8,128)(2,1)S(1)}, bf16[128,1024]{1,0:T(8,128)(2,1)S(1)}, u32[]{:S(2)}, u32[]{:S(2)}) collective-permute-start(bf16[128,1024]{1,0:T(8,128)(2,1)S(1)} %collective-permute-done.12.refs_3_), channel_id=1, source_target_pairs={{0,2},{1,5},{4,0},{5,9},{8,4},{9,13},{12,8},{13,15},{14,12},{15,11... | collective-permute-start | bytes 786440 | tf_op jit(solution)/shard_map/ppermute | solution.py:238
  39.9 17.4 %collective-permute-start.15 = (f32[128,2048]{1,0:T(8,128)S(1)}, f32[128,2048]{1,0:T(8,128)S(1)}, u32[]{:S(2)}, u32[]{:S(2)}) collective-permute-start(f32[128,2048]{1,0:T(8,128)S(1)} %get-tuple-element.45), channel_id=1, source_target_pairs={{0,1},{1,0},{2,3},{3,2},{4,5},{5,4},{6,7},{7,6},{8,9},{9,8},{10,11... | collective-permute-start | bytes 3145736 | tf_op jit(solution)/shard_map/ppermute | solution.py:265
  40.0 8.2 %collective-permute-start.2 = (bf16[128,1024]{1,0:T(8,128)(2,1)S(1)}, bf16[128,1024]{1,0:T(8,128)(2,1)S(1)}, u32[]{:S(2)}, u32[]{:S(2)}) collective-permute-start(bf16[128,1024]{1,0:T(8,128)(2,1)S(1)} %collective-permute-done.1.refs_0_), channel_id=1, source_target_pairs={{0,4},{1,3},{4,8},{5,1},{8,12},{9,5},{12,14},{13,9},{14,10},{15,13... | collective-permute-start | bytes 786440 | tf_op jit(solution)/shard_map/ppermute | solution.py:238
  41.9 8.7 %collective-permute-start.10 = (bf16[128,1024]{1,0:T(8,128)(2,1)S(1)}, bf16[128,1024]{1,0:T(8,128)(2,1)S(1)}, u32[]{:S(2)}, u32[]{:S(2)}) collective-permute-start(bf16[128,1024]{1,0:T(8,128)(2,1)S(1)} %collective-permute-done.9.refs_2_), channel_id=1, source_target_pairs={{0,2},{1,5},{4,0},{5,9},{8,4},{9,13},{12,8},{13,15},{14,12},{15,11... | collective-permute-start | bytes 786440 | tf_op jit(solution)/shard_map/ppermute | solution.py:238
  48.1 6.7 %collective-permute-start.3 = (bf16[128,1024]{1,0:T(8,128)(2,1)S(1)}, bf16[128,1024]{1,0:T(8,128)(2,1)S(1)}, u32[]{:S(2)}, u32[]{:S(2)}) collective-permute-start(bf16[128,1024]{1,0:T(8,128)(2,1)S(1)} %collective-permute-done.2.refs_0_), channel_id=1, source_target_pairs={{0,4},{1,3},{4,8},{5,1},{8,12},{9,5},{12,14},{13,9},{14,10},{15,13... | collective-permute-start | bytes 786440 | tf_op jit(solution)/shard_map/ppermute | solution.py:238
  50.6 6.7 %collective-permute-start.7 = (bf16[128,1024]{1,0:T(8,128)(2,1)S(1)}, bf16[128,1024]{1,0:T(8,128)(2,1)S(1)}, u32[]{:S(2)}, u32[]{:S(2)}) collective-permute-start(bf16[128,1024]{1,0:T(8,128)(2,1)S(1)} %collective-permute-done.6.refs_0_), channel_id=1, source_target_pairs={{0,5},{1,2},{4,9},{5,0},{8,13},{9,4},{12,15},{13,8},{14,11},{15,12... | collective-permute-start | bytes 786440 | tf_op jit(solution)/shard_map/ppermute | solution.py:238
  50.6 6.7 %copy-start = (bf16[384,2048]{1,0:T(8,128)(2,1)S(1)}, bf16[384,2048]{1,0:T(8,128)(2,1)}, u32[]{:S(2)}) copy-start(bf16[384,2048]{1,0:T(8,128)(2,1)} %refs_6_.1) | copy-start | bytes 4718596
  61.1 7.2 %collective-permute-start.17 = (f32[4,96,128]{2,1,0:T(8,128)S(1)}, f32[4,96,128]{2,1,0:T(8,128)S(1)}, u32[]{:S(2)}, u32[]{:S(2)}) collective-permute-start(f32[4,96,128]{2,1,0:T(8,128)S(1)} %dynamic-slice_bitcast_fusion), channel_id=1, source_target_pairs={{0,2},{2,0},{4,6},{6,4},{8,10},{10,8},{12,14},{14,12},{1,3},{3,1},... | collective-permute-start | bytes 589832 | tf_op jit(solution)/shard_map/ppermute | solution.py:219
  68.3 6.3 %collective-permute-start.18 = (f32[96,128]{1,0:T(8,128)S(1)}, f32[96,128]{1,0:T(8,128)S(1)}, u32[]{:S(2)}, u32[]{:S(2)}) collective-permute-start(f32[96,128]{1,0:T(8,128)S(1)} %get-tuple-element.53), channel_id=1, source_target_pairs={{0,4},{2,6},{4,8},{6,10},{8,12},{10,14},{12,0},{14,2},{1,5},{3,7},... | collective-permute-start | bytes 147464 | tf_op jit(solution)/shard_map/ppermute | solution.py:223
  70.4 6.3 %collective-permute-start.19 = (f32[96,128]{1,0:T(8,128)S(1)}, f32[96,128]{1,0:T(8,128)S(1)}, u32[]{:S(2)}, u32[]{:S(2)}) collective-permute-start(f32[96,128]{1,0:T(8,128)S(1)} %get-tuple-element.55), channel_id=1, source_target_pairs={{0,8},{2,10},{4,12},{6,14},{8,0},{10,2},{12,4},{14,6},{1,9},{3,11}... | collective-permute-start | bytes 147464 | tf_op jit(solution)/shard_map/ppermute | solution.py:223
  73.2 4.1 %collective-permute-start.20 = (f32[96,128]{1,0:T(8,128)S(1)}, f32[96,128]{1,0:T(8,128)S(1)}, u32[]{:S(2)}, u32[]{:S(2)}) collective-permute-start(f32[96,128]{1,0:T(8,128)S(1)} %get-tuple-element.54), channel_id=1, source_target_pairs={{0,12},{2,14},{4,0},{6,2},{8,4},{10,6},{12,8},{14,10},{1,13},{3,15... | collective-permute-start | bytes 147464 | tf_op jit(solution)/shard_map/ppermute | solution.py:223
